TPU v7x, 128 devices: a whole 4x4x4 slice. The times are simulated.
128 devices in a mesh: row: 8 (over z, core), col: 8 (over x, y_hi), depth: 2 (over y_lo).
Axes of the slice: x: 4, y: 4 (y_hi: 2, y_lo: 2; y = y_hi * 2 + y_lo), z: 4, core: 2. Of those that a mesh axis runs over, the one named last changes fastest.
Arguments:
- amplitudes: bfloat16 [616, 616, 1024], P('col', 'row', 'depth'), may hold values from -6 to 6
- ladder_ints: bfloat16 [616, 616, 1024], P('col', 'row', 'depth'), may hold values from -0.013671875 to 0.013671875
- cycle_ints: bfloat16 [616, 32, 2048], P('row', None, 'col'), may hold values from -0.0625 to 0.0625
- ladder_source: float32 [1024, 1024], P(('row', 'col'), 'depth'), may hold values from -6 to 6
- cycle_source: float32 [616, 32, 2048], P('col', 'depth', 'row'), may hold values from -6 to 6
- occ_energy: float32 [32], replicated, may hold values from -2 to -0.4
- virt_energy: float32 [616], replicated, may hold values from 0.2 to 3
- pair_energy: float32 [1024], P(('row', 'col')), may hold values from 0.4 to 6
- slice_energy: float32 [64], replicated, may hold values from 0.2 to 3
Outputs:
- ladder_new: float32 [1024, 1024], P(('row', 'col'), 'depth')
- cycle_new: float32 [616, 32, 2048], P('col', 'depth', 'row')
All inputs are finite; a program needn't handle non-finite values.
Results may differ from a plain program's by a relative error of at most 0.0003.
Values may be sent and summed in bfloat16 or wider, within the bound.
No kernel may reach another device: no remote copies, remote signals or barrier semaphores. Data moves between devices by JAX's collectives and lax.ppermute only.
A program may use at most 128 MiB of HBM per device.

v0:
```python
import jax
import jax.numpy as jnp
from jax import lax
from jax.sharding import PartitionSpec as P


def body(
    amplitudes,
    ladder_ints,
    cycle_ints,
    ladder_source,
    cycle_source,
    occ_energy,
    virt_energy,
    pair_energy,
    slice_energy,
):
    virt_col, virt_row, pair_occ = amplitudes.shape
    occ_all = occ_energy.shape[0]
    occ_dev = pair_occ // occ_all
    inner = virt_col * virt_row
    flat_amp = amplitudes.reshape(inner, pair_occ)
    piece = lax.all_gather(ladder_ints, "depth", axis=2, tiled=True)
    partial_sum = lax.dot_general(
        piece.reshape(inner, piece.shape[2]),
        flat_amp,
        (((0,), (0,)), ((), ())),
        preferred_element_type=jnp.float32,
    )
    ladder_sum = lax.psum_scatter(partial_sum, ("row", "col"), scatter_dimension=0, tiled=True)
    occ_mine = lax.dynamic_slice_in_dim(occ_energy, lax.axis_index("depth") * occ_dev, occ_dev)
    occ_pairs = (occ_mine[:, None] + occ_energy[None, :]).reshape(pair_occ)
    ladder_den = occ_pairs[None, :] - pair_energy[:, None]
    ladder_new = (ladder_source + ladder_sum) / ladder_den
    slice_size = slice_energy.shape[0]
    cycle_amp = (
        amplitudes.reshape(virt_col, virt_row, occ_dev, occ_all)
        .transpose(0, 2, 1, 3)
        .reshape(virt_col * occ_dev, virt_row * occ_all)
    )
    piece = lax.all_gather(cycle_ints, "col", axis=2, tiled=True)
    cycle_part = jnp.dot(
        cycle_amp,
        piece.reshape(virt_row * occ_all, piece.shape[2]),
        preferred_element_type=jnp.float32,
    )
    cycle_part = cycle_part.reshape(virt_col, occ_dev, occ_all * slice_size)
    cycle_sum = lax.psum_scatter(cycle_part, "row", scatter_dimension=2, tiled=True)
    occ_share = cycle_sum.shape[2] // slice_size
    occ_rows = lax.dynamic_slice_in_dim(occ_energy, lax.axis_index("row") * occ_share, occ_share)
    virt_mine = lax.dynamic_slice_in_dim(virt_energy, lax.axis_index("col") * virt_col, virt_col)
    jb_part = (occ_rows[:, None] - slice_energy[None, :]).reshape(occ_share * slice_size)
    cycle_den = occ_mine[None, :, None] - virt_mine[:, None, None] + jb_part[None, None, :]
    cycle_new = (cycle_source + cycle_sum) / cycle_den
    return (ladder_new, cycle_new)


def solution(mesh):
    placed = (
        P("col", "row", "depth"),
        P("col", "row", "depth"),
        P("row", None, "col"),
        P(("row", "col"), "depth"),
        P("col", "depth", "row"),
        P(),
        P(),
        P(("row", "col")),
        P(),
    )
    return jax.shard_map(
        body,
        mesh=mesh,
        in_specs=placed,
        out_specs=(P(("row", "col"), "depth"), P("col", "depth", "row")),
        check_vma=False,
    )
```

profile of v0, /device:TPU:0, one launch (start us, length us, event | category | flops | bytes accessed | tf_op | source)
XLA Modules:
  0.0 716.0 jit_solution(5468249073596840638)
XLA Ops:
  7.2 0.0 all-gather.3.cloned.1.call-start
  7.2 0.7 all-gather.3.cloned.1.call-update
  7.9 0.0 all-gather.5.cloned.1.call-start
  8.0 0.5 copy-done
  8.5 1.8 copy.14
  10.2 0.0 all-gather.5.cloned.1.call-update
  10.2 0.0 reduce-scatter.3.cloned.1.call-start
  10.3 11.4 %copy.13 = bf16[77,77,512]{1,2,0:T(8,128)(2,1)} copy(bf16[77,77,512]{2,1,0:T(8,128)(2,1)} %param.9) | data formatting | bytes 12142592 | tf_op args[0]
  21.7 145.9 %all-gather.3.cloned.1.call-done = bf16[77,77,1024]{2,1,0:T(8,128)(2,1)} async-done(((bf16[77,77,512]{2,1,0:T(8,128)(2,1)}), bf16[77,77,1024]{2,1,0:T(8,128)(2,1)}) %all-gather.3.cloned.1.call-update) | async-done | bytes 12142608 | tf_op jit(solution)/shard_map/all_gather | solution.py:23
  167.6 12.8 %convolution_bitcast_fusion = f32[1024,512]{1,0:T(8,128)} fusion(bf16[77,77,1024]{2,1,0:T(8,128)(2,1)} %all-gather.3.cloned.1.call-done, bf16[77,77,512]{2,1,0:T(8,128)(2,1)} %param.9), kind=kOutput, calls=%fused_computation.4 | convolution fusion | flops 6217007104 | bytes 20311040 | tf_op jit(solution)/shard_map/dot_general | solution.py:24
  180.3 0.0 reduce-scatter.3.cloned.1.call-update
  180.4 0.0 reduce-scatter.5.cloned.1.call-start
  180.4 132.2 %all-gather.5.cloned.1.call-done = bf16[77,32,2048]{2,0,1:T(8,128)(2,1)} async-done(((bf16[77,32,256]{2,0,1:T(8,128)(2,1)}), bf16[77,32,2048]{2,0,1:T(8,128)(2,1)}) %all-gather.5.cloned.1.call-update) | async-done | bytes 10092560 | tf_op jit(solution)/shard_map/all_gather | solution.py:41
  312.7 34.6 %fusion.3 = f32[77,16,2048]{2,1,0:T(8,128)} fusion(bf16[77,32,2048]{2,0,1:T(8,128)(2,1)} %all-gather.5.cloned.1.call-done, bf16[77,16,77,32]{2,3,1,0:T(8,128)(2,1)} %bitcast.15), kind=kOutput, calls=%fused_computation.3 | convolution fusion | flops 12434014208 | bytes 26256384 | tf_op jit(solution)/shard_map/dot_general | solution.py:42
  347.3 0.0 copy-start.3
  347.3 0.0 copy-start.1
  347.3 0.0 reduce-scatter.5.cloned.1.call-update
  347.3 0.6 copy-done.4
  347.9 0.1 dynamic_slice.9
  348.0 0.1 broadcast_add_fusion
  348.1 0.1 add.57
  348.2 0.1 dynamic_slice.11
  348.2 0.0 copy-done.5
  348.2 0.1 broadcast_subtract_fusion.1
  348.3 0.1 sub.60
  348.4 0.8 dynamic_slice.10
  349.2 0.1 broadcast_subtract_fusion
  349.2 300.9 %reduce-scatter.3.cloned.1.call-done = f32[16,512]{1,0:T(8,128)} async-done(((f32[1024,512]{1,0:T(8,128)}), f32[16,512]{1,0:T(8,128)}) %reduce-scatter.3.cloned.1.call-update) | async-done | bytes 32784 | tf_op jit(solution)/shard_map/reduce_scatter | solution.py:30
  650.1 0.0 copy-done.2
  650.1 1.5 subtract_divide_fusion
  651.6 55.3 %reduce-scatter.5.cloned.1.call-done = f32[77,16,256]{2,1,0:T(8,128)} async-done(((f32[77,16,2048]{2,1,0:T(8,128)}), f32[77,16,256]{2,1,0:T(8,128)}) %reduce-scatter.5.cloned.1.call-update) | async-done | bytes 1261584 | tf_op jit(solution)/shard_map/reduce_scatter | solution.py:48
  706.9 2.6 add_divide_fusion
  (6 shorter events, 0.0 us)
Async XLA Ops:
  7.2 1.3 copy-start
  7.2 160.4 %all-gather.3.cloned.1.call-start = ((), (), s32[]{:S(2)}) async-start(), calls=%async_computation.2 | async-start | bytes 18923520 | tf_op jit(solution)/shard_map/all_gather | solution.py:23
  7.9 304.8 %all-gather.5.cloned.1.call-start = ((), (), s32[]{:S(2)}) async-start(), calls=%async_computation.4 | async-start | bytes 11796480 | tf_op jit(solution)/shard_map/all_gather | solution.py:41
  10.2 639.9 %reduce-scatter.3.cloned.1.call-start = ((), (), s32[]{:S(2)}) async-start(), calls=%async_computation.3 | async-start | bytes 2129920 | tf_op jit(solution)/shard_map/reduce_scatter | solution.py:30
  180.4 526.5 %reduce-scatter.5.cloned.1.call-start = ((), (), s32[]{:S(2)}) async-start(), calls=%async_computation.5 | async-start | bytes 11354112 | tf_op jit(solution)/shard_map/reduce_scatter | solution.py:48
  347.3 0.7 copy-start.4
  347.3 1.0 copy-start.5
  347.3 302.8 %copy-start.2 = (f32[16,512]{1,0:T(8,128)S(1)}, f32[16,512]{1,0:T(8,128)}, u32[]{:S(2)}) copy-start(f32[16,512]{1,0:T(8,128)} %param.12) | copy-start | bytes 98308
  347.3 302.8 %copy-start.3 = (f32[16]{0:T(128)S(1)}, f32[16]{0:T(128)}, u32[]{:S(2)}) copy-start(f32[16]{0:T(128)} %param.16) | copy-start | bytes 196
  347.3 359.6 %copy-start.1 = (f32[77,16,256]{2,1,0:T(8,128)S(1)}, f32[77,16,256]{2,1,0:T(8,128)}, u32[]{:S(2)}) copy-start(f32[77,16,256]{2,1,0:T(8,128)} %param.13) | copy-start | bytes 3784708
Sparse Core Ops, SparseCore 0:
  9.7 157.8 all-gather.2
  169.8 142.8 all-gather.4
  315.0 335.0 reduce-scatter.2
  652.5 54.3 reduce-scatter.4
where the time goes:
time: 717 us; the launch traced here: 716 us
  waiting for transfers between devices  635 us (89%)
  matrix products  47.4 us (7%)
  local copies, waits for them, and re-layouts  15.3 us (2%)
  between operations  13.8 us (2%)
    reduce_scatter x1, waiting for transfers between devices, body(): lax.psum_scatter(partial_sum, ('row', 'col'), scatter_dimension=0, tiled=...  301 us
    all_gather x1, waiting for transfers between devices, body(): piece = lax.all_gather(ladder_ints, 'depth', axis=2, tiled=True)  146 us
    all_gather x1, waiting for transfers between devices, body(): piece = lax.all_gather(cycle_ints, 'col', axis=2, tiled=True)  132 us
    reduce_scatter x1, waiting for transfers between devices, body(): lax.psum_scatter(cycle_part, 'row', scatter_dimension=2, tiled=True)  55.3 us
    dot_general x1, matrix products, body(): jnp.dot(cycle_amp, piece.reshape(virt_row * occ_all, piece.shape[2]), pre...  34.6 us
  transfers between devices with their start and end apart: 4, of which 4 were waited for; matrix products, arithmetic and copies ran while one was open for 9% of the time, Pallas kernels for 0%

commit v1 on v0

v1 whole, which is shorter than its diff:
```python
import jax
import jax.numpy as jnp
from jax import lax
from jax.experimental import pallas as pl
from jax.experimental.pallas import tpu as pltpu
from jax.sharding import PartitionSpec as P

NZ, NCORE = 4, 2
NX, NHI = 4, 2
LANES = 128
OCC = 32
SMALL = pl.CostEstimate(flops=1000, bytes_accessed=1000, transcendentals=0)
F32 = jnp.float32

SWAP_DEPTH = [(0, 1), (1, 0)]
SWAP_CORE = [(i, i ^ 1) for i in range(NZ * NCORE)]
SWAP_HI = [(i, i ^ 1) for i in range(NX * NHI)]
ACROSS = [(i, i ^ 3) for i in range(NX * NHI * 2)]


def shift_z(s):
    return [(z * NCORE + c, (z + s) % NZ * NCORE + c) for z in range(NZ) for c in range(NCORE)]


def shift_x(s):
    return [(x * NHI + h, (x + s) % NX * NHI + h) for x in range(NX) for h in range(NHI)]


def across_x(s):
    pairs = []
    for i, j in ACROSS:
        x, rest = divmod(j, NHI * 2)
        pairs.append((i, (x + s) % NX * NHI * 2 + rest))
    return pairs


def after(value, *others):
    return lax.optimization_barrier((value,) + others)[0]


def pick(value, index, axis):
    return lax.dynamic_index_in_dim(value, index, axis, keepdims=False)


def four_way(blocks, mine, axis_name, shift):
    kept = pick(blocks, mine, 0)
    got = [lax.ppermute(pick(blocks, (mine + s) % 4, 0), axis_name, shift(s)) for s in (1, 2, 3)]
    return kept + got[0] + got[1] + got[2]


def two_way(blocks, mine, axis_name, swap):
    return pick(blocks, mine, 0) + lax.ppermute(pick(blocks, 1 - mine, 0), axis_name, swap)


def reduce_col(part, x, hi):
    n, rows, pair_occ = part.shape
    keep = rows // (NX * NHI)
    v = part.reshape(n, NX, NHI, keep, pair_occ).transpose(1, 2, 0, 3, 4)
    v = four_way(v, x, "col", shift_x)
    return two_way(v, hi, "col", SWAP_HI)


def amp_kernel(src, dst, rows_in, rows_out):
    n, virt, lanes = src.shape
    occ_dev = dst.shape[1]
    per_tile = LANES // OCC
    groups = rows_in.shape[1] // per_tile
    piece = lax.broadcasted_iota(jnp.int32, (groups, LANES), 1) // OCC
    rows_in[...] = jnp.zeros_like(rows_in)

    def one(a, carry):
        for i4 in range(lanes // LANES):
            rows_in[i4, :virt, :] = src[a, :, i4 * LANES : (i4 + 1) * LANES].astype(F32)
        for i4 in range(lanes // LANES):
            v = [rows_in[i4, pl.ds(c, groups, stride=per_tile), :] for c in range(per_tile)]
            for i in range(per_tile):
                r = v[0] if i == 0 else pltpu.roll(v[0], (-i * OCC) % LANES, 1)
                for c in range(1, per_tile):
                    w = v[c] if c == i else pltpu.roll(v[c], ((c - i) * OCC) % LANES, 1)
                    r = jnp.where(piece == c, w, r)
                rows_out[pl.ds(i4 * per_tile + i, groups, stride=occ_dev), :] = r
        for g in range(groups):
            width = min(LANES, virt * OCC - g * LANES)
            tile = rows_out[g * occ_dev : (g + 1) * occ_dev, :].astype(jnp.bfloat16)
            dst[a, :, g * LANES : g * LANES + width] = tile[:, :width]
        return carry

    lax.fori_loop(0, n, one, 0)


def cycle_layout(amplitudes, occ_dev):
    virt_col, virt_row, pair_occ = amplitudes.shape
    step = 7 if virt_col % 7 == 0 else 1
    padded = pl.cdiv(virt_row * OCC, LANES) * LANES // OCC
    out = pl.pallas_call(
        amp_kernel,
        grid=(virt_col // step,),
        in_specs=[pl.BlockSpec((step, virt_row, pair_occ), lambda g: (g, 0, 0))],
        out_specs=pl.BlockSpec((step, occ_dev, virt_row * OCC), lambda g: (g, 0, 0)),
        out_shape=jax.ShapeDtypeStruct((virt_col, occ_dev, virt_row * OCC), amplitudes.dtype),
        scratch_shapes=[
            pltpu.VMEM((pair_occ // LANES, padded, LANES), F32),
            pltpu.VMEM((padded * OCC // LANES * occ_dev, LANES), F32),
        ],
        cost_estimate=SMALL,
    )(amplitudes)
    return out.reshape(virt_col * occ_dev, virt_row * OCC)


def cycle_kernel(order, amp, *refs):
    blocks, out = refs[:-1], refs[-1]
    step = pl.program_id(0)
    hi = order[1]
    for s in range(NX):

        @pl.when(step == s)
        def _():
            b = jnp.concatenate([blocks[2 * s][...], blocks[2 * s + 1][...]], axis=1)
            r = jnp.dot(amp[...], b, preferred_element_type=F32)
            out[:, pl.ds(pl.multiple_of(hi * LANES, LANES), LANES)] = r[:, :LANES]
            out[:, pl.ds(pl.multiple_of((1 - hi) * LANES, LANES), LANES)] = r[:, LANES:]


def cycle_dot(order, amp, blocks):
    m, k = amp.shape
    grid_spec = pltpu.PrefetchScalarGridSpec(
        num_scalar_prefetch=1,
        grid=(NX,),
        in_specs=[pl.BlockSpec((m, k), lambda s, o: (0, 0))]
        + [pl.BlockSpec((k, LANES), lambda s, o: (0, 0)) for _ in blocks],
        out_specs=pl.BlockSpec((m, NHI * LANES), lambda s, o: (0, (o[0] + s) % NX)),
    )
    return pl.pallas_call(
        cycle_kernel,
        grid_spec=grid_spec,
        out_shape=jax.ShapeDtypeStruct((m, NX * NHI * LANES), F32),
        compiler_params=pltpu.CompilerParams(vmem_limit_bytes=50 << 20),
        cost_estimate=SMALL,
    )(order, amp, *blocks)


def gather_near(own):
    across = lax.ppermute(own, ("col", "depth"), ACROSS)
    own_l = lax.ppermute(own, "col", shift_x(1))
    own_r = lax.ppermute(own, "col", shift_x(-1))
    own_again = after(own, own_l, own_r)
    across_l = lax.ppermute(own_again, ("col", "depth"), across_x(1))
    across_r = lax.ppermute(own_again, ("col", "depth"), across_x(-1))
    return own, across, own_l, own_r, across_l, across_r


def gather_far(near, gate):
    own, across, own_l, own_r, across_l, across_r = near
    own_far = lax.ppermute(after(own_l, gate), "col", shift_x(1))
    across_far = lax.ppermute(after(across_r, gate), "col", shift_x(-1))
    return [own, across, own_r, across_r, own_far, across_far, own_l, across_l]


def body(
    amplitudes,
    ladder_ints,
    cycle_ints,
    ladder_source,
    cycle_source,
    occ_energy,
    virt_energy,
    pair_energy,
    slice_energy,
):
    virt_col, virt_row, pair_occ = amplitudes.shape
    occ_all = occ_energy.shape[0]
    occ_dev = pair_occ // occ_all
    slice_size = slice_energy.shape[0]
    row = lax.axis_index("row")
    col = lax.axis_index("col")
    depth = lax.axis_index("depth")
    z, core = row // NCORE, row % NCORE
    x, hi = col // NHI, col % NHI

    chunks = ladder_ints.shape[2] // LANES
    got, pieces = [], []
    for c in range(chunks):
        source = ladder_ints
        if c >= 1:
            source = after(source, pieces[c - 1])
        if c >= 2:
            source = after(source, got[c - 2])
        pieces.append(lax.slice_in_dim(source, c * LANES, (c + 1) * LANES, axis=2))
        got.append(lax.ppermute(pieces[c], "depth", SWAP_DEPTH))

    halves = cycle_ints.shape[2] // LANES
    near = []
    for h in range(halves):
        source = after(cycle_ints, pieces[h], *near[h - 1][:1]) if h else after(cycle_ints, pieces[0])
        own = lax.slice_in_dim(source, h * LANES, (h + 1) * LANES, axis=2)
        near.append(gather_near(own.reshape(virt_row * occ_all, LANES)))

    def ladder_dot(ints):
        return lax.dot_general(ints, amplitudes, (((0, 1), (0, 1)), ((), ())), preferred_element_type=F32)

    own_dot = ladder_dot(ladder_ints)
    own_part = own_dot.reshape(chunks, LANES, pair_occ)

    cycle_amp = cycle_layout(amplitudes, occ_dev)
    order = jnp.stack([x, hi]).astype(jnp.int32)
    cycle_sums = []
    gate = (cycle_amp, own_dot)
    for h in range(halves):
        blocks = gather_far(near[h], gate[0])
        order = after(order, *gate, got[h], *(v for n in near for v in n[1:4]))
        part = cycle_dot(order, cycle_amp, blocks)
        gate = (part,)
        part = part.reshape(virt_col, occ_dev, NX * NHI * LANES)
        cycle_sums.append(lax.psum_scatter(part, "row", scatter_dimension=2, tiled=True))

    other = [ladder_dot(g)[None] for g in got]
    early = reduce_col(jnp.concatenate([own_part] + other[:-1], axis=0), x, hi)
    late = reduce_col(other[-1], x, hi)
    mine, rest = early[:chunks], jnp.concatenate([early[chunks:], late], axis=0)
    both = jnp.where(depth == 0, jnp.concatenate([mine, rest], 0), jnp.concatenate([rest, mine], 0))
    v = both.reshape(NZ, NCORE, both.shape[1], pair_occ).transpose(1, 0, 2, 3)
    v = two_way(v, core, "row", SWAP_CORE)
    ladder_sum = four_way(v, z, "row", shift_z)

    occ_mine = lax.dynamic_slice_in_dim(occ_energy, depth * occ_dev, occ_dev)
    occ_pairs = (occ_mine[:, None] + occ_energy[None, :]).reshape(pair_occ)
    ladder_den = occ_pairs[None, :] - pair_energy[:, None]
    ladder_new = (ladder_source + ladder_sum) / ladder_den

    cycle_sum = jnp.concatenate(cycle_sums, axis=2)
    occ_share = cycle_sum.shape[2] // slice_size
    occ_rows = lax.dynamic_slice_in_dim(occ_energy, row * occ_share, occ_share)
    virt_mine = lax.dynamic_slice_in_dim(virt_energy, col * virt_col, virt_col)
    jb_part = (occ_rows[:, None] - slice_energy[None, :]).reshape(occ_share * slice_size)
    cycle_den = occ_mine[None, :, None] - virt_mine[:, None, None] + jb_part[None, None, :]
    cycle_new = (cycle_source + cycle_sum) / cycle_den
    return (ladder_new, cycle_new)


def solution(mesh):
    placed = (
        P("col", "row", "depth"),
        P("col", "row", "depth"),
        P("row", None, "col"),
        P(("row", "col"), "depth"),
        P("col", "depth", "row"),
        P(),
        P(),
        P(("row", "col")),
        P(),
    )
    return jax.shard_map(
        body,
        mesh=mesh,
        in_specs=placed,
        out_specs=(P(("row", "col"), "depth"), P("col", "depth", "row")),
        check_vma=False,
    )
```

time: 717 us -> 292 us (0.41)
  waiting for transfers between devices: 635 us -> 145 us
  starting transfers between devices: 0.16 us -> 49.8 us
  Pallas kernels: 0 us -> 42.6 us
  matrix products: 47.4 us -> 18.1 us
    reduce_scatter x2, waiting for transfers between devices: 356 us -> 0.01 us  [body(): lax.psum_scatter(part, 'row', scatter_dimension=2, tiled=True)]
    all_gather x2 -> x0, waiting for transfers between devices: 278 us -> none  [the longest x1 146 us: body(): piece = lax.all_gather(ladder_ints, 'depth', axis=2, tiled=True)]
    ppermute x0 -> x30, waiting for transfers between devices: none -> 145 us  [the longest x4 45.9 us: body(): got.append(lax.ppermute(pieces[c], 'depth', SWAP_DEPTH))]
    ppermute x0 -> x30, starting transfers between devices: none -> 49.7 us  [the longest x9 18.3 us: four_way(): lax.ppermute(pick(blocks, (mine + s) % 4, 0), axis_name, shift(s))]
    pallas_call x0 -> x3, Pallas kernels: none -> 42.6 us  [the longest x2 25.4 us: cycle_dot(): pl.pallas_call(cycle_kernel, grid_spec=grid_spec, out_shape=jax.ShapeDtyp...]
    dot_general x2 -> x5, matrix products: 47.4 us -> 18.1 us  [ladder_dot(): lax.dot_general(ints, amplitudes, (((0, 1), (0, 1)), ((), ())), preferred...]
    unnamed x14 -> x32, local copies, waits for them, and re-layouts: 14.2 us -> 0.68 us
    slice x0 -> x8, local copies, waits for them, and re-layouts: none -> 11.1 us  [the longest x4 10.8 us: body(): pieces.append(lax.slice_in_dim(source, c * LANES, (c + 1) * LANES, axis=2))]
  transfers between devices with their start and end apart: 4 -> 32, of which waited for: 4 -> 16; matrix products, arithmetic and copies ran while one was open for 9% -> 11% of each run, Pallas kernels for 0% -> 10%
where the time goes in v1:
time: 292 us; the launch traced here: 291 us
  waiting for transfers between devices  145 us (50%)
  starting transfers between devices  49.8 us (17%)
  Pallas kernels  42.6 us (15%)
  matrix products  18.1 us (6%)
  local copies, waits for them, and re-layouts  14.8 us (5%)
  between operations  14.3 us (5%)
  other arithmetic  6.54 us (2%)
    ppermute x4, waiting for transfers between devices, body(): got.append(lax.ppermute(pieces[c], 'depth', SWAP_DEPTH))  45.9 us
    pallas_call x2, Pallas kernels, cycle_dot(): pl.pallas_call(cycle_kernel, grid_spec=grid_spec, out_shape=jax.ShapeDtyp...  25.4 us
    ppermute x2, waiting for transfers between devices, gather_near(): across_r = lax.ppermute(own_again, ('col', 'depth'), across_x(-1))  24.7 us
    ppermute x9, waiting for transfers between devices, four_way(): lax.ppermute(pick(blocks, (mine + s) % 4, 0), axis_name, shift(s))  20.4 us
    ppermute x2, waiting for transfers between devices, gather_far(): own_far = lax.ppermute(after(own_l, gate), 'col', shift_x(1))  19.7 us
    ppermute x9, starting transfers between devices, four_way(): lax.ppermute(pick(blocks, (mine + s) % 4, 0), axis_name, shift(s))  18.3 us
    dot_general x5, matrix products, ladder_dot(): lax.dot_general(ints, amplitudes, (((0, 1), (0, 1)), ((), ())), preferred...  18.1 us
    pallas_call x1, Pallas kernels, cycle_layout(): pl.pallas_call(amp_kernel, grid=(virt_col // step,), in_specs=[pl.BlockSp...  17.2 us
  transfers between devices with their start and end apart: 32, of which 16 were waited for; matrix products, arithmetic and copies ran while one was open for 11% of the time, Pallas kernels for 10%

profile of v1, /device:TPU:0, one launch (start us, length us, event | category | flops | bytes accessed | tf_op | source)
XLA Modules:
  0.0 291.2 jit_solution(12249543000423569817)
XLA Ops:
  7.2 2.8 slice.25
  11.7 1.7 collective-permute-start.18
  15.1 2.2 collective-permute-start.16
  17.3 2.7 slice.26
  20.0 7.2 %collective-permute-done.17.refs_6_ = bf16[2464,128]{1,0:T(8,128)(2,1)S(1)} collective-permute-done((bf16[2464,128]{1,0:T(8,128)(2,1)S(1)}, bf16[2464,128]{1,0:T(8,128)(2,1)S(1)}, u32[]{:S(2)}, u32[]{:S(2)}) %collective-permute-start.17) | collective-permute-done | bytes 630816 | tf_op jit(solution)/shard_map/ppermute | solution.py:144
  27.4 5.4 %collective-permute-start.22 = (bf16[2464,128]{1,0:T(8,128)(2,1)S(1)}, bf16[2464,128]{1,0:T(8,128)(2,1)}, u32[]{:S(2)}, u32[]{:S(2)}) collective-permute-start(bf16[2464,128]{1,0:T(8,128)(2,1)S(1)} %bitcast.108), channel_id=1, source_target_pairs={{0,15},{1,14},{2,13},{3,12},{4,3},{5,2},{6,1},{7,0},{8,7},{9,6},{1... | collective-permute-start | bytes 1892360 | tf_op jit(solution)/shard_map/ppermute | solution.py:148
  33.1 17.2 %shard_map.104 = bf16[77,16,2464]{2,1,0:T(8,128)(2,1)} custom-call(bf16[77,77,512]{2,1,0:T(8,128)(2,1)} %src.1), custom_call_target="tpu_custom_call" | custom-call | flops 1000 | bytes 1000 | tf_op jit(solution)/shard_map/pallas_call | solution.py:95
  50.3 3.2 %collective-permute-start.21 = (bf16[2464,128]{1,0:T(8,128)(2,1)S(1)}, bf16[2464,128]{1,0:T(8,128)(2,1)S(1)}, u32[]{:S(2)}, u32[]{:S(2)}) collective-permute-start(bf16[2464,128]{1,0:T(8,128)(2,1)S(1)} %bitcast.101), channel_id=1, source_target_pairs={{0,12},{2,14},{4,0},{6,2},{8,4},{10,6},{12,8},{14,10},{1,13},{3,15... | collective-permute-start | bytes 1892360 | tf_op jit(solution)/shard_map/ppermute | solution.py:145
  54.9 17.0 %collective-permute-done.19.refs_1_ = bf16[2464,128]{1,0:T(8,128)(2,1)S(1)} collective-permute-done((bf16[2464,128]{1,0:T(8,128)(2,1)S(1)}, bf16[2464,128]{1,0:T(8,128)(2,1)S(1)}, u32[]{:S(2)}, u32[]{:S(2)}) %collective-permute-start.19) | collective-permute-done | bytes 630816 | tf_op jit(solution)/shard_map/ppermute | solution.py:143
  72.9 2.5 collective-permute-start.24
  75.5 14.6 %collective-permute-done.23.refs_4_ = bf16[2464,128]{1,0:T(8,128)(2,1)} collective-permute-done((bf16[2464,128]{1,0:T(8,128)(2,1)}, bf16[2464,128]{1,0:T(8,128)(2,1)}, u32[]{:S(2)}, u32[]{:S(2)}) %collective-permute-start.23) | collective-permute-done | bytes 630816 | tf_op jit(solution)/shard_map/ppermute | solution.py:154
  90.1 13.1 %shard_map.105 = f32[1232,1024]{1,0:T(8,128)} custom-call(s32[2]{0:T(128)S(1)} %pad_add_fusion.order, bf16[1232,2464]{1,0:T(8,128)(2,1)} %bitcast.113, bf16[2464,128]{1,0:T(8,128)(2,1)S(1)} %bitcast.110, bf16[2464,128]{1,0:T(8,128)(2,1)} %collective-permute-done.16.refs_1_, bf16[2464,128]{1,0:T(8,128)(2,1)S(1)} %collective-permute-done.18.refs_2_, ...), custom_call_target="tpu_custom_call" | custom-call | flops 1000 | bytes 1000 | tf_op jit(solution)/shard_map/pallas_call | solution.py:133
  103.4 4.8 %collective-permute-start.26 = (bf16[2464,128]{1,0:T(8,128)(2,1)S(1)}, bf16[2464,128]{1,0:T(8,128)(2,1)S(1)}, u32[]{:S(2)}, u32[]{:S(2)}) collective-permute-start(bf16[2464,128]{1,0:T(8,128)(2,1)S(1)} %bitcast.102), channel_id=1, source_target_pairs={{0,15},{1,14},{2,13},{3,12},{4,3},{5,2},{6,1},{7,0},{8,7},{9,6},{1... | collective-permute-start | bytes 1892360 | tf_op jit(solution)/shard_map/ppermute | solution.py:148
  108.7 24.7 %collective-permute-done.26.refs_3_ = bf16[2464,128]{1,0:T(8,128)(2,1)S(1)} collective-permute-done((bf16[2464,128]{1,0:T(8,128)(2,1)S(1)}, bf16[2464,128]{1,0:T(8,128)(2,1)S(1)}, u32[]{:S(2)}, u32[]{:S(2)}) %collective-permute-start.26) | collective-permute-done | bytes 630816 | tf_op jit(solution)/shard_map/ppermute | solution.py:148
  134.2 5.2 %collective-permute-done.1 = bf16[77,77,128]{2,1,0:T(8,128)(2,1)S(1)} collective-permute-done((bf16[77,77,128]{2,1,0:T(8,128)(2,1)}, bf16[77,77,128]{2,1,0:T(8,128)(2,1)S(1)}, u32[]{:S(2)}, u32[]{:S(2)}) %collective-permute-start.1) | collective-permute-done | bytes 1517856 | tf_op jit(solution)/shard_map/ppermute | solution.py:189
  139.4 5.1 %collective-permute-done.27.refs_4_ = bf16[2464,128]{1,0:T(8,128)(2,1)S(1)} collective-permute-done((bf16[2464,128]{1,0:T(8,128)(2,1)}, bf16[2464,128]{1,0:T(8,128)(2,1)S(1)}, u32[]{:S(2)}, u32[]{:S(2)}) %collective-permute-start.27) | collective-permute-done | bytes 630816 | tf_op jit(solution)/shard_map/ppermute | solution.py:154
  145.9 12.3 %shard_map.106 = f32[1232,1024]{1,0:T(8,128)} custom-call(s32[2]{0:T(128)S(1)} %pad_add_fusion.order, bf16[1232,2464]{1,0:T(8,128)(2,1)} %bitcast.114, bf16[2464,128]{1,0:T(8,128)(2,1)S(1)} %bitcast.104, bf16[2464,128]{1,0:T(8,128)(2,1)S(1)} %collective-permute-done.19.refs_1_, bf16[2464,128]{1,0:T(8,128)(2,1)S(1)} %collective-permute-done.21.refs_2_, ...), custom_call_target="tpu_custom_call" | custom-call | flops 1000 | bytes 1000 | tf_op jit(solution)/shard_map/pallas_call | solution.py:133
  158.2 2.7 slice.27
  160.9 2.6 slice.28
  164.8 9.2 %fusion.9 = f32[512,512,1]{1,0,2:T(8,128)} fusion(bf16[77,77,512]{2,1,0:T(8,128)(2,1)} %param.10, bf16[77,77,512]{2,1,0:T(8,128)(2,1)} %src.1), kind=kOutput, calls=%fused_computation.34 | convolution fusion | flops 3108503552 | bytes 13191168 | tf_op jit(solution)/shard_map/dot_general | solution.py:199
  175.8 4.4 %fusion.11 = f32[128,512,1]{1,0,2:T(8,128)S(1)} fusion(bf16[77,77,128]{2,1,0:T(8,128)(2,1)S(1)} %copy-done.1, bf16[77,77,512]{2,1,0:T(8,128)(2,1)} %src.1), kind=kOutput, calls=%fused_computation.36 | convolution fusion | flops 777125888 | bytes 7851264 | tf_op jit(solution)/shard_map/dot_general | solution.py:199
  180.2 2.5 fusion.10
  182.6 18.6 %collective-permute-done.7 = bf16[77,77,128]{2,1,0:T(8,128)(2,1)S(1)} collective-permute-done((bf16[77,77,128]{2,1,0:T(8,128)(2,1)}, bf16[77,77,128]{2,1,0:T(8,128)(2,1)S(1)}, u32[]{:S(2)}, u32[]{:S(2)}) %collective-permute-start.7) | collective-permute-done | bytes 1517856 | tf_op jit(solution)/shard_map/ppermute | solution.py:189
  203.0 4.8 %collective-permute-start.10 = (f32[2,1,16,512]{3,2,1,0:T(8,128)S(1)}, f32[2,1,16,512]{3,2,1,0:T(8,128)S(1)}, u32[]{:S(2)}, u32[]{:S(2)}) collective-permute-start(f32[2,1,16,512]{3,2,1,0:T(8,128)S(1)} %get-tuple-element.36), channel_id=1, source_target_pairs={{0,12},{2,14},{4,0},{6,2},{8,4},{10,6},{12,8},{14,10},{1,13},{3,15... | collective-permute-start | bytes 196616 | tf_op jit(solution)/shard_map/ppermute | solution.py:47
  208.6 22.1 %collective-permute-done.2 = bf16[77,77,128]{2,1,0:T(8,128)(2,1)S(1)} collective-permute-done((bf16[77,77,128]{2,1,0:T(8,128)(2,1)}, bf16[77,77,128]{2,1,0:T(8,128)(2,1)S(1)}, u32[]{:S(2)}, u32[]{:S(2)}) %collective-permute-start.2) | collective-permute-done | bytes 1517856 | tf_op jit(solution)/shard_map/ppermute | solution.py:189
  233.1 6.1 %collective-permute-start.5 = (f32[2,7,16,512]{3,2,0,1:T(8,128)}, f32[2,7,16,512]{3,2,0,1:T(8,128)S(1)}, u32[]{:S(2)}, u32[]{:S(2)}) collective-permute-start(f32[2,7,16,512]{3,2,0,1:T(8,128)} %get-tuple-element.33), channel_id=1, source_target_pairs={{0,12},{2,14},{4,0},{6,2},{8,4},{10,6},{12,8},{14,10},{1,13},{3,15... | collective-permute-start | bytes 1376264 | tf_op jit(solution)/shard_map/ppermute | solution.py:47
  243.3 13.1 %collective-permute-done.5 = f32[2,7,16,512]{3,2,0,1:T(8,128)S(1)} collective-permute-done((f32[2,7,16,512]{3,2,0,1:T(8,128)}, f32[2,7,16,512]{3,2,0,1:T(8,128)S(1)}, u32[]{:S(2)}, u32[]{:S(2)}) %collective-permute-start.5) | collective-permute-done | bytes 458784 | tf_op jit(solution)/shard_map/ppermute | solution.py:47
  256.4 3.3 %collective-permute-done.3 = f32[2,7,16,512]{3,2,0,1:T(8,128)} collective-permute-done((f32[2,7,16,512]{3,2,0,1:T(8,128)S(1)}, f32[2,7,16,512]{3,2,0,1:T(8,128)}, u32[]{:S(2)}, u32[]{:S(2)}) %collective-permute-start.3) | collective-permute-done | bytes 458784 | tf_op jit(solution)/shard_map/ppermute | solution.py:47
  262.3 7.3 %collective-permute-done.6 = f32[7,16,512]{2,1,0:T(8,128)S(1)} collective-permute-done((f32[7,16,512]{2,1,0:T(8,128)S(1)}, f32[7,16,512]{2,1,0:T(8,128)S(1)}, u32[]{:S(2)}, u32[]{:S(2)}) %collective-permute-start.6) | collective-permute-done | bytes 229408 | tf_op jit(solution)/shard_map/ppermute | solution.py:52
  271.2 4.4 %collective-permute-start.15 = (f32[16,512]{1,0:T(8,128)S(1)}, f32[16,512]{1,0:T(8,128)S(1)}, u32[]{:S(2)}, u32[]{:S(2)}) collective-permute-start(f32[16,512]{1,0:T(8,128)S(1)} %get-tuple-element.39), channel_id=1, source_target_pairs={{0,96},{16,112},{32,0},{48,16},{64,32},{80,48},{96,64},{112,80},{1... | collective-permute-start | bytes 98312 | tf_op jit(solution)/shard_map/ppermute | solution.py:47
  277.2 3.9 %collective-permute-done.14 = f32[16,512]{1,0:T(8,128)S(1)} collective-permute-done((f32[16,512]{1,0:T(8,128)S(1)}, f32[16,512]{1,0:T(8,128)S(1)}, u32[]{:S(2)}, u32[]{:S(2)}) %collective-permute-start.14) | collective-permute-done | bytes 32800 | tf_op jit(solution)/shard_map/ppermute | solution.py:47
  281.8 2.6 fusion
  (107 shorter events, 27.7 us)
Async XLA Ops:
  7.2 274.6 %reduce-scatter.3.cloned.1.call-start = ((), (), s32[]{:S(2)}) async-start(), calls=%async_computation.2 | async-start | bytes 5677056 | tf_op jit(solution)/shard_map/reduce_scatter | solution.py:214
  10.1 17.1 %collective-permute-start.17 = (bf16[2464,128]{1,0:T(8,128)(2,1)S(1)}, bf16[2464,128]{1,0:T(8,128)(2,1)S(1)}, u32[]{:S(2)}, u32[]{:S(2)}) collective-permute-start(bf16[2464,128]{1,0:T(8,128)(2,1)S(1)} %bitcast.105), channel_id=1, source_target_pairs={{0,4},{2,6},{4,8},{6,10},{8,12},{10,14},{12,0},{14,2},{1,5},{3,7},... | collective-permute-start | bytes 1892360 | tf_op jit(solution)/shard_map/ppermute | solution.py:144
  11.7 15.7 %collective-permute-start.18 = (bf16[2464,128]{1,0:T(8,128)(2,1)S(1)}, bf16[2464,128]{1,0:T(8,128)(2,1)S(1)}, u32[]{:S(2)}, u32[]{:S(2)}) collective-permute-start(bf16[2464,128]{1,0:T(8,128)(2,1)S(1)} %bitcast.106), channel_id=1, source_target_pairs={{0,12},{2,14},{4,0},{6,2},{8,4},{10,6},{12,8},{14,10},{1,13},{3,15... | collective-permute-start | bytes 1892360 | tf_op jit(solution)/shard_map/ppermute | solution.py:145
  13.4 62.1 %collective-permute-start = (bf16[77,77,128]{2,1,0:T(8,128)(2,1)}, bf16[77,77,128]{2,1,0:T(8,128)(2,1)}, u32[]{:S(2)}, u32[]{:S(2)}) collective-permute-start(bf16[77,77,128]{2,1,0:T(8,128)(2,1)} %slice.25), channel_id=1, source_target_pairs={{0,1},{1,0},{2,3},{3,2},{4,5},{5,4},{6,7},{7,6},{8,9},{9,8},{10,11... | collective-permute-start | bytes 4553480 | tf_op jit(solution)/shard_map/ppermute | solution.py:189
  15.1 38.5 %collective-permute-start.16 = (bf16[2464,128]{1,0:T(8,128)(2,1)S(1)}, bf16[2464,128]{1,0:T(8,128)(2,1)}, u32[]{:S(2)}, u32[]{:S(2)}) collective-permute-start(bf16[2464,128]{1,0:T(8,128)(2,1)S(1)} %bitcast.107), channel_id=1, source_target_pairs={{0,3},{1,2},{2,1},{3,0},{4,7},{5,6},{6,5},{7,4},{8,11},{9,10},{10,... | collective-permute-start | bytes 1892360 | tf_op jit(solution)/shard_map/ppermute | solution.py:143
  27.4 22.9 %collective-permute-start.22 = (bf16[2464,128]{1,0:T(8,128)(2,1)S(1)}, bf16[2464,128]{1,0:T(8,128)(2,1)}, u32[]{:S(2)}, u32[]{:S(2)}) collective-permute-start(bf16[2464,128]{1,0:T(8,128)(2,1)S(1)} %bitcast.108), channel_id=1, source_target_pairs={{0,15},{1,14},{2,13},{3,12},{4,3},{5,2},{6,1},{7,0},{8,7},{9,6},{1... | collective-permute-start | bytes 1892360 | tf_op jit(solution)/shard_map/ppermute | solution.py:148
  33.0 39.0 %collective-permute-start.19 = (bf16[2464,128]{1,0:T(8,128)(2,1)S(1)}, bf16[2464,128]{1,0:T(8,128)(2,1)S(1)}, u32[]{:S(2)}, u32[]{:S(2)}) collective-permute-start(bf16[2464,128]{1,0:T(8,128)(2,1)S(1)} %bitcast.99), channel_id=1, source_target_pairs={{0,3},{1,2},{2,1},{3,0},{4,7},{5,6},{6,5},{7,4},{8,11},{9,10},{10,... | collective-permute-start | bytes 1892360 | tf_op jit(solution)/shard_map/ppermute | solution.py:143
  33.1 39.8 %collective-permute-start.20 = (bf16[2464,128]{1,0:T(8,128)(2,1)S(1)}, bf16[2464,128]{1,0:T(8,128)(2,1)}, u32[]{:S(2)}, u32[]{:S(2)}) collective-permute-start(bf16[2464,128]{1,0:T(8,128)(2,1)S(1)} %bitcast.100), channel_id=1, source_target_pairs={{0,4},{2,6},{4,8},{6,10},{8,12},{10,14},{12,0},{14,2},{1,5},{3,7},... | collective-permute-start | bytes 1892360 | tf_op jit(solution)/shard_map/ppermute | solution.py:144
  50.3 25.2 %collective-permute-start.21 = (bf16[2464,128]{1,0:T(8,128)(2,1)S(1)}, bf16[2464,128]{1,0:T(8,128)(2,1)S(1)}, u32[]{:S(2)}, u32[]{:S(2)}) collective-permute-start(bf16[2464,128]{1,0:T(8,128)(2,1)S(1)} %bitcast.101), channel_id=1, source_target_pairs={{0,12},{2,14},{4,0},{6,2},{8,4},{10,6},{12,8},{14,10},{1,13},{3,15... | collective-permute-start | bytes 1892360 | tf_op jit(solution)/shard_map/ppermute | solution.py:145
  53.5 36.6 %collective-permute-start.25 = (bf16[2464,128]{1,0:T(8,128)(2,1)S(1)}, bf16[2464,128]{1,0:T(8,128)(2,1)}, u32[]{:S(2)}, u32[]{:S(2)}) collective-permute-start(bf16[2464,128]{1,0:T(8,128)(2,1)S(1)} %bitcast.109), channel_id=1, source_target_pairs={{0,7},{1,6},{2,5},{3,4},{4,11},{5,10},{6,9},{7,8},{8,15},{9,14},{1... | collective-permute-start | bytes 1892360 | tf_op jit(solution)/shard_map/ppermute | solution.py:147
  71.9 18.2 %collective-permute-start.23 = (bf16[2464,128]{1,0:T(8,128)(2,1)}, bf16[2464,128]{1,0:T(8,128)(2,1)}, u32[]{:S(2)}, u32[]{:S(2)}) collective-permute-start(bf16[2464,128]{1,0:T(8,128)(2,1)} %copy-done.5), channel_id=1, source_target_pairs={{0,4},{2,6},{4,8},{6,10},{8,12},{10,14},{12,0},{14,2},{1,5},{3,7},... | collective-permute-start | bytes 1892360 | tf_op jit(solution)/shard_map/ppermute | solution.py:154
  72.9 17.2 %collective-permute-start.24 = (bf16[2464,128]{1,0:T(8,128)(2,1)}, bf16[2464,128]{1,0:T(8,128)(2,1)}, u32[]{:S(2)}, u32[]{:S(2)}) collective-permute-start(bf16[2464,128]{1,0:T(8,128)(2,1)} %collective-permute-done.22.refs_3_), channel_id=1, source_target_pairs={{0,12},{2,14},{4,0},{6,2},{8,4},{10,6},{12,8},{14,10},{1,13},{3,15... | collective-permute-start | bytes 1892360 | tf_op jit(solution)/shard_map/ppermute | solution.py:155
  103.2 178.6 %reduce-scatter.5.cloned.1.call-start = ((), (), s32[]{:S(2)}) async-start(), calls=%async_computation.3 | async-start | bytes 5677056 | tf_op jit(solution)/shard_map/reduce_scatter | solution.py:214
  103.3 36.2 %collective-permute-start.1 = (bf16[77,77,128]{2,1,0:T(8,128)(2,1)}, bf16[77,77,128]{2,1,0:T(8,128)(2,1)S(1)}, u32[]{:S(2)}, u32[]{:S(2)}) collective-permute-start(bf16[77,77,128]{2,1,0:T(8,128)(2,1)} %slice.26), channel_id=1, source_target_pairs={{0,1},{1,0},{2,3},{3,2},{4,5},{5,4},{6,7},{7,6},{8,9},{9,8},{10,11... | collective-permute-start | bytes 4553480 | tf_op jit(solution)/shard_map/ppermute | solution.py:189
  103.4 30.0 %collective-permute-start.26 = (bf16[2464,128]{1,0:T(8,128)(2,1)S(1)}, bf16[2464,128]{1,0:T(8,128)(2,1)S(1)}, u32[]{:S(2)}, u32[]{:S(2)}) collective-permute-start(bf16[2464,128]{1,0:T(8,128)(2,1)S(1)} %bitcast.102), channel_id=1, source_target_pairs={{0,15},{1,14},{2,13},{3,12},{4,3},{5,2},{6,1},{7,0},{8,7},{9,6},{1... | collective-permute-start | bytes 1892360 | tf_op jit(solution)/shard_map/ppermute | solution.py:148
  108.1 31.3 %collective-permute-start.29 = (bf16[2464,128]{1,0:T(8,128)(2,1)S(1)}, bf16[2464,128]{1,0:T(8,128)(2,1)S(1)}, u32[]{:S(2)}, u32[]{:S(2)}) collective-permute-start(bf16[2464,128]{1,0:T(8,128)(2,1)S(1)} %bitcast.103), channel_id=1, source_target_pairs={{0,7},{1,6},{2,5},{3,4},{4,11},{5,10},{6,9},{7,8},{8,15},{9,14},{1... | collective-permute-start | bytes 1892360 | tf_op jit(solution)/shard_map/ppermute | solution.py:147
  108.1 36.4 %collective-permute-start.27 = (bf16[2464,128]{1,0:T(8,128)(2,1)}, bf16[2464,128]{1,0:T(8,128)(2,1)S(1)}, u32[]{:S(2)}, u32[]{:S(2)}) collective-permute-start(bf16[2464,128]{1,0:T(8,128)(2,1)} %collective-permute-done.20.refs_6_), channel_id=1, source_target_pairs={{0,4},{2,6},{4,8},{6,10},{8,12},{10,14},{12,0},{14,2},{1,5},{3,7},... | collective-permute-start | bytes 1892360 | tf_op jit(solution)/shard_map/ppermute | solution.py:154
  133.4 12.4 %collective-permute-start.28 = (bf16[2464,128]{1,0:T(8,128)(2,1)S(1)}, bf16[2464,128]{1,0:T(8,128)(2,1)S(1)}, u32[]{:S(2)}, u32[]{:S(2)}) collective-permute-start(bf16[2464,128]{1,0:T(8,128)(2,1)S(1)} %collective-permute-done.26.refs_3_), channel_id=1, source_target_pairs={{0,12},{2,14},{4,0},{6,2},{8,4},{10,6},{12,8},{14,10},{1,13},{3,15... | collective-permute-start | bytes 1892360 | tf_op jit(solution)/shard_map/ppermute | solution.py:155
  163.6 37.6 %collective-permute-start.7 = (bf16[77,77,128]{2,1,0:T(8,128)(2,1)}, bf16[77,77,128]{2,1,0:T(8,128)(2,1)S(1)}, u32[]{:S(2)}, u32[]{:S(2)}) collective-permute-start(bf16[77,77,128]{2,1,0:T(8,128)(2,1)} %slice.28), channel_id=1, source_target_pairs={{0,1},{1,0},{2,3},{3,2},{4,5},{5,4},{6,7},{7,6},{8,9},{9,8},{10,11... | collective-permute-start | bytes 4553480 | tf_op jit(solution)/shard_map/ppermute | solution.py:189
  175.0 55.8 %collective-permute-start.2 = (bf16[77,77,128]{2,1,0:T(8,128)(2,1)}, bf16[77,77,128]{2,1,0:T(8,128)(2,1)S(1)}, u32[]{:S(2)}, u32[]{:S(2)}) collective-permute-start(bf16[77,77,128]{2,1,0:T(8,128)(2,1)} %slice.27), channel_id=1, source_target_pairs={{0,1},{1,0},{2,3},{3,2},{4,5},{5,4},{6,7},{7,6},{8,9},{9,8},{10,11... | collective-permute-start | bytes 4553480 | tf_op jit(solution)/shard_map/ppermute | solution.py:189
  203.0 36.2 %collective-permute-start.10 = (f32[2,1,16,512]{3,2,1,0:T(8,128)S(1)}, f32[2,1,16,512]{3,2,1,0:T(8,128)S(1)}, u32[]{:S(2)}, u32[]{:S(2)}) collective-permute-start(f32[2,1,16,512]{3,2,1,0:T(8,128)S(1)} %get-tuple-element.36), channel_id=1, source_target_pairs={{0,12},{2,14},{4,0},{6,2},{8,4},{10,6},{12,8},{14,10},{1,13},{3,15... | collective-permute-start | bytes 196616 | tf_op jit(solution)/shard_map/ppermute | solution.py:47
  207.8 33.0 %collective-permute-start.9 = (f32[2,1,16,512]{3,2,1,0:T(8,128)}, f32[2,1,16,512]{3,2,1,0:T(8,128)S(1)}, u32[]{:S(2)}, u32[]{:S(2)}) collective-permute-start(f32[2,1,16,512]{3,2,1,0:T(8,128)} %get-tuple-element.37), channel_id=1, source_target_pairs={{0,8},{2,10},{4,12},{6,14},{8,0},{10,2},{12,4},{14,6},{1,9},{3,11}... | collective-permute-start | bytes 196616 | tf_op jit(solution)/shard_map/ppermute | solution.py:47
  207.8 33.6 %collective-permute-start.8 = (f32[2,1,16,512]{3,2,1,0:T(8,128)}, f32[2,1,16,512]{3,2,1,0:T(8,128)}, u32[]{:S(2)}, u32[]{:S(2)}) collective-permute-start(f32[2,1,16,512]{3,2,1,0:T(8,128)} %get-tuple-element.35), channel_id=1, source_target_pairs={{0,4},{2,6},{4,8},{6,10},{8,12},{10,14},{12,0},{14,2},{1,5},{3,7},... | collective-permute-start | bytes 196616 | tf_op jit(solution)/shard_map/ppermute | solution.py:47
  233.1 23.3 %collective-permute-start.5 = (f32[2,7,16,512]{3,2,0,1:T(8,128)}, f32[2,7,16,512]{3,2,0,1:T(8,128)S(1)}, u32[]{:S(2)}, u32[]{:S(2)}) collective-permute-start(f32[2,7,16,512]{3,2,0,1:T(8,128)} %get-tuple-element.33), channel_id=1, source_target_pairs={{0,12},{2,14},{4,0},{6,2},{8,4},{10,6},{12,8},{14,10},{1,13},{3,15... | collective-permute-start | bytes 1376264 | tf_op jit(solution)/shard_map/ppermute | solution.py:47
  239.2 17.2 %collective-permute-start.4 = (f32[2,7,16,512]{3,2,0,1:T(8,128)}, f32[2,7,16,512]{3,2,0,1:T(8,128)S(1)}, u32[]{:S(2)}, u32[]{:S(2)}) collective-permute-start(f32[2,7,16,512]{3,2,0,1:T(8,128)} %get-tuple-element.34), channel_id=1, source_target_pairs={{0,8},{2,10},{4,12},{6,14},{8,0},{10,2},{12,4},{14,6},{1,9},{3,11}... | collective-permute-start | bytes 1376264 | tf_op jit(solution)/shard_map/ppermute | solution.py:47
  239.2 20.5 %collective-permute-start.3 = (f32[2,7,16,512]{3,2,0,1:T(8,128)S(1)}, f32[2,7,16,512]{3,2,0,1:T(8,128)}, u32[]{:S(2)}, u32[]{:S(2)}) collective-permute-start(f32[2,7,16,512]{3,2,0,1:T(8,128)S(1)} %get-tuple-element.32), channel_id=1, source_target_pairs={{0,4},{2,6},{4,8},{6,10},{8,12},{10,14},{12,0},{14,2},{1,5},{3,7},... | collective-permute-start | bytes 1376264 | tf_op jit(solution)/shard_map/ppermute | solution.py:47
  242.3 20.0 %collective-permute-start.11 = (f32[1,16,512]{2,1,0:T(8,128)S(1)}, f32[1,16,512]{2,1,0:T(8,128)S(1)}, u32[]{:S(2)}, u32[]{:S(2)}) collective-permute-start(f32[1,16,512]{2,1,0:T(8,128)S(1)} %dynamic-slice_bitcast_fusion.11), channel_id=1, source_target_pairs={{0,2},{2,0},{4,6},{6,4},{8,10},{10,8},{12,14},{14,12},{1,3},{3,1},... | collective-permute-start | bytes 98312 | tf_op jit(solution)/shard_map/ppermute | solution.py:52
  260.9 8.6 %collective-permute-start.6 = (f32[7,16,512]{2,1,0:T(8,128)S(1)}, f32[7,16,512]{2,1,0:T(8,128)S(1)}, u32[]{:S(2)}, u32[]{:S(2)}) collective-permute-start(f32[7,16,512]{2,1,0:T(8,128)S(1)} %dynamic-slice_bitcast_fusion.3), channel_id=1, source_target_pairs={{0,2},{2,0},{4,6},{6,4},{8,10},{10,8},{12,14},{14,12},{1,3},{3,1},... | collective-permute-start | bytes 688136 | tf_op jit(solution)/shard_map/ppermute | solution.py:52
  269.7 1.4 collective-permute-start.12
  271.2 6.0 %collective-permute-start.15 = (f32[16,512]{1,0:T(8,128)S(1)}, f32[16,512]{1,0:T(8,128)S(1)}, u32[]{:S(2)}, u32[]{:S(2)}) collective-permute-start(f32[16,512]{1,0:T(8,128)S(1)} %get-tuple-element.39), channel_id=1, source_target_pairs={{0,96},{16,112},{32,0},{48,16},{64,32},{80,48},{96,64},{112,80},{1... | collective-permute-start | bytes 98312 | tf_op jit(solution)/shard_map/ppermute | solution.py:47
  275.6 5.5 %collective-permute-start.14 = (f32[16,512]{1,0:T(8,128)S(1)}, f32[16,512]{1,0:T(8,128)S(1)}, u32[]{:S(2)}, u32[]{:S(2)}) collective-permute-start(f32[16,512]{1,0:T(8,128)S(1)} %get-tuple-element.40), channel_id=1, source_target_pairs={{0,64},{16,80},{32,96},{48,112},{64,0},{80,16},{96,32},{112,48},{1... | collective-permute-start | bytes 98312 | tf_op jit(solution)/shard_map/ppermute | solution.py:47
  275.6 5.5 %collective-permute-start.13 = (f32[16,512]{1,0:T(8,128)S(1)}, f32[16,512]{1,0:T(8,128)S(1)}, u32[]{:S(2)}, u32[]{:S(2)}) collective-permute-start(f32[16,512]{1,0:T(8,128)S(1)} %get-tuple-element.38), channel_id=1, source_target_pairs={{0,32},{16,48},{32,64},{48,80},{64,96},{80,112},{96,0},{112,16},{1... | collective-permute-start | bytes 98312 | tf_op jit(solution)/shard_map/ppermute | solution.py:47
  (16 other events, 191.3 us)
Sparse Core Ops, SparseCore 0:
  103.3 41.7 reduce-scatter.2
  158.4 42.0 reduce-scatter.4

commit v2 on v1

--- a/solution.py
+++ b/solution.py
@@ -1,3 +1,5 @@
+import functools
+
 import jax
 import jax.numpy as jnp
 from jax import lax
@@ -16,6 +18,7 @@
 SWAP_CORE = [(i, i ^ 1) for i in range(NZ * NCORE)]
 SWAP_HI = [(i, i ^ 1) for i in range(NX * NHI)]
 ACROSS = [(i, i ^ 3) for i in range(NX * NHI * 2)]
+LONG = pl.CostEstimate(flops=20_000_000_000, bytes_accessed=1000, transcendentals=0)
 
 
 def shift_z(s):
@@ -38,6 +41,10 @@
     return lax.optimization_barrier((value,) + others)[0]
 
 
+def corner(value):
+    return lax.slice(value, (0,) * value.ndim, (1,) * (value.ndim - 2) + (8, LANES))
+
+
 def pick(value, index, axis):
     return lax.dynamic_index_in_dim(value, index, axis, keepdims=False)
 
@@ -48,15 +55,54 @@
     return kept + got[0] + got[1] + got[2]
 
 
+def ring_row(keep, send, gate):
+    got = {r: keep[r] + lax.ppermute(after(send[r], gate), "row", SWAP_CORE) for r in (2, 1, 3, 0)}
+    half = keep.shape[1] // 2
+    up = lax.ppermute(got[2][:half], "row", shift_z(1))
+    down = lax.ppermute(got[2][half:], "row", shift_z(3))
+    right = jnp.concatenate([got[1][:half] + up, got[1][half:]], axis=0)
+    left = jnp.concatenate([got[3][:half], got[3][half:] + down], axis=0)
+    below = lax.ppermute(right, "row", shift_z(1))
+    above = lax.ppermute(left, "row", shift_z(3))
+    return got[0] + below + above, (below, above)
+
+
 def two_way(blocks, mine, axis_name, swap):
     return pick(blocks, mine, 0) + lax.ppermute(pick(blocks, 1 - mine, 0), axis_name, swap)
 
 
-def reduce_col(part, x, hi):
+def turn_kernel(start, src, *refs):
+    dst = refs[-src.shape[0] :]
+    for s, d in enumerate(dst):
+        d[...] = src[(start[0] + s) % len(dst)]
+
+
+def turn(blocks, start, gates):
+    n = blocks.shape[0]
+    one = jax.ShapeDtypeStruct(blocks.shape[1:], blocks.dtype)
+    return pl.pallas_call(
+        turn_kernel,
+        in_specs=[
+            pl.BlockSpec(memory_space=pltpu.SMEM),
+            pl.BlockSpec(memory_space=pltpu.VMEM),
+        ]
+        + [pl.BlockSpec(memory_space=pl.ANY)] * len(gates),
+        out_specs=[pl.BlockSpec(memory_space=pltpu.VMEM)] * n,
+        out_shape=[one] * n,
+        cost_estimate=LONG,
+    )(start.reshape(1).astype(jnp.int32), blocks, *gates)
+
+
+def reduce_col(part, x, hi, gates=()):
     n, rows, pair_occ = part.shape
     keep = rows // (NX * NHI)
     v = part.reshape(n, NX, NHI, keep, pair_occ).transpose(1, 2, 0, 3, 4)
-    v = four_way(v, x, "col", shift_x)
+    if gates:
+        kept, *sent = turn(v, x, gates)
+        got = [lax.ppermute(b, "col", shift_x(s + 1)) for s, b in enumerate(sent)]
+        v = kept + got[0] + got[1] + got[2]
+    else:
+        v = four_way(v, x, "col", shift_x)
     return two_way(v, hi, "col", SWAP_HI)
 
 
@@ -107,52 +153,60 @@
     return out.reshape(virt_col * occ_dev, virt_row * OCC)
 
 
-def cycle_kernel(order, amp, *refs):
-    blocks, out = refs[:-1], refs[-1]
+def cycle_kernel(order, amp, *refs, blocks_in):
+    blocks, (keep, send) = refs[:blocks_in], refs[-NCORE:]
     step = pl.program_id(0)
-    hi = order[1]
+    swapped = order[1] != order[2]
     for s in range(NX):
 
         @pl.when(step == s)
         def _():
-            b = jnp.concatenate([blocks[2 * s][...], blocks[2 * s + 1][...]], axis=1)
-            r = jnp.dot(amp[...], b, preferred_element_type=F32)
-            out[:, pl.ds(pl.multiple_of(hi * LANES, LANES), LANES)] = r[:, :LANES]
-            out[:, pl.ds(pl.multiple_of((1 - hi) * LANES, LANES), LANES)] = r[:, LANES:]
-
-
-def cycle_dot(order, amp, blocks):
+            for i in range(NHI):
+                r = jnp.dot(amp[...], blocks[NHI * s + i][...], preferred_element_type=F32)
+
+                @pl.when(swapped)
+                def _():
+                    (send, keep)[i][...] = r
+
+                @pl.when(jnp.logical_not(swapped))
+                def _():
+                    (keep, send)[i][...] = r
+
+
+def cycle_dot(order, amp, blocks, gates):
     m, k = amp.shape
+    n = blocks[0].shape[1]
+    whole = lambda s, o: (0, 0)
+    once = pl.Buffered(1)
     grid_spec = pltpu.PrefetchScalarGridSpec(
         num_scalar_prefetch=1,
         grid=(NX,),
-        in_specs=[pl.BlockSpec((m, k), lambda s, o: (0, 0))]
-        + [pl.BlockSpec((k, LANES), lambda s, o: (0, 0)) for _ in blocks],
-        out_specs=pl.BlockSpec((m, NHI * LANES), lambda s, o: (0, (o[0] + s) % NX)),
+        in_specs=[pl.BlockSpec((m, k), whole, pipeline_mode=once)]
+        + [pl.BlockSpec((k, n), whole, pipeline_mode=once) for _ in blocks]
+        + [pl.BlockSpec(memory_space=pl.ANY) for _ in gates],
+        out_specs=[pl.BlockSpec((pl.Squeezed(), m, n), lambda s, o: ((o[0] + s + NZ - o[3]) % NZ, 0, 0))] * NCORE,
     )
     return pl.pallas_call(
-        cycle_kernel,
+        functools.partial(cycle_kernel, blocks_in=len(blocks)),
         grid_spec=grid_spec,
-        out_shape=jax.ShapeDtypeStruct((m, NX * NHI * LANES), F32),
+        out_shape=[jax.ShapeDtypeStruct((NZ, m, n), F32)] * NCORE,
         compiler_params=pltpu.CompilerParams(vmem_limit_bytes=50 << 20),
         cost_estimate=SMALL,
-    )(order, amp, *blocks)
-
-
-def gather_near(own):
+    )(order, amp, *blocks, *gates)
+
+
+def gather_cycle(own, gate):
+    half = own.shape[0] // 2
     across = lax.ppermute(own, ("col", "depth"), ACROSS)
     own_l = lax.ppermute(own, "col", shift_x(1))
     own_r = lax.ppermute(own, "col", shift_x(-1))
-    own_again = after(own, own_l, own_r)
-    across_l = lax.ppermute(own_again, ("col", "depth"), across_x(1))
-    across_r = lax.ppermute(own_again, ("col", "depth"), across_x(-1))
-    return own, across, own_l, own_r, across_l, across_r
-
-
-def gather_far(near, gate):
-    own, across, own_l, own_r, across_l, across_r = near
-    own_far = lax.ppermute(after(own_l, gate), "col", shift_x(1))
-    across_far = lax.ppermute(after(across_r, gate), "col", shift_x(-1))
+    far_a = lax.ppermute(after(own_l, gate)[:half], "col", shift_x(1))
+    far_b = lax.ppermute(after(own_r, gate)[half:], "col", shift_x(-1))
+    own_far = jnp.concatenate([far_a, far_b], axis=0)
+    again = after(across, far_a, far_b)
+    across_l = lax.ppermute(again, "col", shift_x(1))
+    across_r = lax.ppermute(again, "col", shift_x(-1))
+    across_far = lax.ppermute(own_far, ("col", "depth"), ACROSS)
     return [own, across, own_r, across_r, own_far, across_far, own_l, across_l]
 
 
@@ -178,46 +232,32 @@
     x, hi = col // NHI, col % NHI
 
     chunks = ladder_ints.shape[2] // LANES
-    got, pieces = [], []
-    for c in range(chunks):
-        source = ladder_ints
-        if c >= 1:
-            source = after(source, pieces[c - 1])
-        if c >= 2:
-            source = after(source, got[c - 2])
-        pieces.append(lax.slice_in_dim(source, c * LANES, (c + 1) * LANES, axis=2))
-        got.append(lax.ppermute(pieces[c], "depth", SWAP_DEPTH))
-
-    halves = cycle_ints.shape[2] // LANES
-    near = []
-    for h in range(halves):
-        source = after(cycle_ints, pieces[h], *near[h - 1][:1]) if h else after(cycle_ints, pieces[0])
-        own = lax.slice_in_dim(source, h * LANES, (h + 1) * LANES, axis=2)
-        near.append(gather_near(own.reshape(virt_row * occ_all, LANES)))
+    begun = chunks - 1
+    cut = begun * LANES
+    most = lax.slice_in_dim(ladder_ints, 0, cut, axis=2)
+    got_most = lax.ppermute(most, "depth", SWAP_DEPTH)
 
     def ladder_dot(ints):
         return lax.dot_general(ints, amplitudes, (((0, 1), (0, 1)), ((), ())), preferred_element_type=F32)
 
     own_dot = ladder_dot(ladder_ints)
     own_part = own_dot.reshape(chunks, LANES, pair_occ)
-
     cycle_amp = cycle_layout(amplitudes, occ_dev)
-    order = jnp.stack([x, hi]).astype(jnp.int32)
-    cycle_sums = []
-    gate = (cycle_amp, own_dot)
-    for h in range(halves):
-        blocks = gather_far(near[h], gate[0])
-        order = after(order, *gate, got[h], *(v for n in near for v in n[1:4]))
-        part = cycle_dot(order, cycle_amp, blocks)
-        gate = (part,)
-        part = part.reshape(virt_col, occ_dev, NX * NHI * LANES)
-        cycle_sums.append(lax.psum_scatter(part, "row", scatter_dimension=2, tiled=True))
-
-    other = [ladder_dot(g)[None] for g in got]
-    early = reduce_col(jnp.concatenate([own_part] + other[:-1], axis=0), x, hi)
-    late = reduce_col(other[-1], x, hi)
-    mine, rest = early[:chunks], jnp.concatenate([early[chunks:], late], axis=0)
-    both = jnp.where(depth == 0, jnp.concatenate([mine, rest], 0), jnp.concatenate([rest, mine], 0))
+
+    blocks = gather_cycle(cycle_ints.reshape(virt_row * occ_all, cycle_ints.shape[2]), corner(cycle_amp))
+    last = lax.slice_in_dim(after(ladder_ints, blocks[1]), cut, chunks * LANES, axis=2)
+    got_last = lax.ppermute(last, "depth", SWAP_DEPTH)
+    order = jnp.stack([x, hi, core, z]).astype(jnp.int32)
+    keep, send = cycle_dot(order, cycle_amp, blocks, (own_dot,))
+    cycle_sum, cycle_parts = ring_row(keep, send, got_most)
+    cycle_sum = cycle_sum.reshape(virt_col, occ_dev, cycle_ints.shape[2])
+
+    most_part = ladder_dot(after(got_most, corner(keep))).reshape(begun, LANES, pair_occ)
+    last_part = ladder_dot(after(got_last, *cycle_parts)).reshape(chunks - begun, LANES, pair_occ)
+    early = reduce_col(jnp.concatenate([own_part, most_part], axis=0), x, hi)
+    late = reduce_col(last_part, x, hi, gates=(early, *cycle_parts))
+    ladder_mine, rest = early[:chunks], jnp.concatenate([early[chunks:], late], axis=0)
+    both = jnp.where(depth == 0, jnp.concatenate([ladder_mine, rest], 0), jnp.concatenate([rest, ladder_mine], 0))
     v = both.reshape(NZ, NCORE, both.shape[1], pair_occ).transpose(1, 0, 2, 3)
     v = two_way(v, core, "row", SWAP_CORE)
     ladder_sum = four_way(v, z, "row", shift_z)
@@ -227,7 +267,6 @@
     ladder_den = occ_pairs[None, :] - pair_energy[:, None]
     ladder_new = (ladder_source + ladder_sum) / ladder_den
 
-    cycle_sum = jnp.concatenate(cycle_sums, axis=2)
     occ_share = cycle_sum.shape[2] // slice_size
     occ_rows = lax.dynamic_slice_in_dim(occ_energy, row * occ_share, occ_share)
     virt_mine = lax.dynamic_slice_in_dim(virt_energy, col * virt_col, virt_col)

time: 292 us -> 233 us (0.80)
  waiting for transfers between devices: 145 us -> 90.6 us
  starting transfers between devices: 49.8 us -> 33.8 us
  between operations: 14.3 us -> 0.93 us
  Pallas kernels: 42.6 us -> 54.7 us
  other arithmetic: 6.54 us -> 14.6 us
  local copies, waits for them, and re-layouts: 14.8 us -> 19.6 us
    ppermute x18 -> x21, waiting for transfers between devices: 116 us -> 74.5 us  [the longest x1 14.2 us: gather_cycle(): across_r = lax.ppermute(again, 'col', shift_x(-1))]
    ppermute x9 -> x6, waiting for transfers between devices: 20.4 us -> 6.79 us  [four_way(): lax.ppermute(pick(blocks, (mine + s) % 4, 0), axis_name, shift(s))]
    pallas_call x2, Pallas kernels: 25.4 us -> 37.5 us  [the longest x1 35.8 us: cycle_dot(): pl.pallas_call(functools.partial(cycle_kernel, blocks_in=len(blocks)), gr...]
    ppermute x9 -> x6, starting transfers between devices: 18.3 us -> 8.07 us  [four_way(): lax.ppermute(pick(blocks, (mine + s) % 4, 0), axis_name, shift(s))]
    add x0 -> x4, other arithmetic: none -> 7.28 us  [the longest x1 3.81 us: ring_row(): keep[r] + lax.ppermute(after(send[r], gate), 'row', SWAP_CORE)]
    ppermute x18 -> x21, starting transfers between devices: 29.1 us -> 22.7 us  [the longest x1 4.15 us: ring_row(): down = lax.ppermute(got[2][half:], 'row', shift_z(3))]
    squeeze x0 -> x1, local copies, waits for them, and re-layouts: none -> 4.41 us  [ring_row(): send[r]]
    dot_general x5 -> x3, matrix products: 18.1 us -> 17.8 us  [ladder_dot(): lax.dot_general(ints, amplitudes, (((0, 1), (0, 1)), ((), ())), preferred...]
  transfers between devices with their start and end apart: 32 -> 30, of which waited for: 16 -> 19; matrix products, arithmetic and copies ran while one was open for 11% -> 19% of each run, Pallas kernels for 10% -> 24%
where the time goes in v2:
time: 233 us; the launch traced here: 232 us
  waiting for transfers between devices  90.6 us (39%)
  Pallas kernels  54.7 us (23%)
  starting transfers between devices  33.8 us (15%)
  local copies, waits for them, and re-layouts  19.6 us (8%)
  matrix products  17.8 us (8%)
  other arithmetic  14.6 us (6%)
    pallas_call x1, Pallas kernels, cycle_dot(): pl.pallas_call(functools.partial(cycle_kernel, blocks_in=len(blocks)), gr...  35.8 us
    dot_general x3, matrix products, ladder_dot(): lax.dot_general(ints, amplitudes, (((0, 1), (0, 1)), ((), ())), preferred...  17.8 us
    pallas_call x1, Pallas kernels, cycle_layout(): pl.pallas_call(amp_kernel, grid=(virt_col // step,), in_specs=[pl.BlockSp...  17.2 us
    ppermute x1, waiting for transfers between devices, gather_cycle(): across_r = lax.ppermute(again, 'col', shift_x(-1))  14.2 us
    ppermute x1, waiting for transfers between devices, ring_row(): above = lax.ppermute(left, 'row', shift_z(3))  11.3 us
    ppermute x1, waiting for transfers between devices, gather_cycle(): far_b = lax.ppermute(after(own_r, gate)[half:], 'col', shift_x(-1))  10.7 us
    ppermute x3, waiting for transfers between devices, two_way(): lax.ppermute(pick(blocks, 1 - mine, 0), axis_name, swap)  9.3 us
    ppermute x6, starting transfers between devices, four_way(): lax.ppermute(pick(blocks, (mine + s) % 4, 0), axis_name, shift(s))  8.07 us
  transfers between devices with their start and end apart: 30, of which 19 were waited for; matrix products, arithmetic and copies ran while one was open for 19% of the time, Pallas kernels for 24%

profile of v2, /device:TPU:0, one launch (start us, length us, event | category | flops | bytes accessed | tf_op | source)
XLA Modules:
  0.0 232.0 jit_solution(16768276636229691290)
XLA Ops:
  0.6 5.1 %slice.65 = bf16[77,77,384]{2,1,0:T(8,128)(2,1)} slice(bf16[77,77,512]{2,1,0:T(8,128)(2,1)} %param.10), slice={[0:77], [0:77], [0:384]} | slice | bytes 9106944 | tf_op jit(solution)/shard_map/slice | solution.py:237
  7.4 2.8 %collective-permute-start.7 = (bf16[2464,256]{1,0:T(8,128)(2,1)S(1)}, bf16[2464,256]{1,0:T(8,128)(2,1)S(1)}, u32[]{:S(2)}, u32[]{:S(2)}) collective-permute-start(bf16[2464,256]{1,0:T(8,128)(2,1)S(1)} %bitcast.98), channel_id=1, source_target_pairs={{0,12},{2,14},{4,0},{6,2},{8,4},{10,6},{12,8},{14,10},{1,13},{3,15... | collective-permute-start | bytes 3784712 | tf_op jit(solution)/shard_map/ppermute | solution.py:202
  10.1 2.2 collective-permute-start.5
  12.3 17.2 %shard_map.104 = bf16[77,16,2464]{2,1,0:T(8,128)(2,1)} custom-call(bf16[77,77,512]{2,1,0:T(8,128)(2,1)} %src.1), custom_call_target="tpu_custom_call" | custom-call | flops 1000 | bytes 1000 | tf_op jit(solution)/shard_map/pallas_call | solution.py:141
  29.5 7.3 %collective-permute-done.7.refs_2_ = bf16[2464,256]{1,0:T(8,128)(2,1)S(1)} collective-permute-done((bf16[2464,256]{1,0:T(8,128)(2,1)S(1)}, bf16[2464,256]{1,0:T(8,128)(2,1)S(1)}, u32[]{:S(2)}, u32[]{:S(2)}) %collective-permute-start.7) | collective-permute-done | bytes 1261600 | tf_op jit(solution)/shard_map/ppermute | solution.py:202
  37.9 3.7 %collective-permute-start.10 = (bf16[1232,256]{1,0:T(8,128)(2,1)}, bf16[1232,256]{1,0:T(8,128)(2,1)S(1)}, u32[]{:S(2)}, u32[]{:S(2)}) collective-permute-start(bf16[1232,256]{1,0:T(8,128)(2,1)} %slice.69), channel_id=1, source_target_pairs={{0,12},{2,14},{4,0},{6,2},{8,4},{10,6},{12,8},{14,10},{1,13},{3,15... | collective-permute-start | bytes 1892360 | tf_op jit(solution)/shard_map/ppermute | solution.py:204
  43.6 10.7 %collective-permute-done.10 = bf16[1232,256]{1,0:T(8,128)(2,1)S(1)} collective-permute-done((bf16[1232,256]{1,0:T(8,128)(2,1)}, bf16[1232,256]{1,0:T(8,128)(2,1)S(1)}, u32[]{:S(2)}, u32[]{:S(2)}) %collective-permute-start.10) | collective-permute-done | bytes 630816 | tf_op jit(solution)/shard_map/ppermute | solution.py:204
  54.2 5.3 %collective-permute-done.9 = bf16[1232,256]{1,0:T(8,128)(2,1)} collective-permute-done((bf16[1232,256]{1,0:T(8,128)(2,1)}, bf16[1232,256]{1,0:T(8,128)(2,1)}, u32[]{:S(2)}, u32[]{:S(2)}) %collective-permute-start.9) | collective-permute-done | bytes 630816 | tf_op jit(solution)/shard_map/ppermute | solution.py:203
  62.8 2.3 collective-permute-start.12
  65.1 7.7 %fusion.15 = f32[512,512,1]{1,0,2:T(8,128)S(1)} fusion(bf16[77,77,512]{2,1,0:T(8,128)(2,1)} %param.10, bf16[77,77,512]{2,1,0:T(8,128)(2,1)} %src.1), kind=kOutput, calls=%fused_computation.58 | convolution fusion | flops 3108503552 | bytes 13191168 | tf_op jit(solution)/shard_map/dot_general | solution.py:241
  72.8 14.2 %collective-permute-done.11.refs_3_ = bf16[2464,256]{1,0:T(8,128)(2,1)S(1)} collective-permute-done((bf16[2464,256]{1,0:T(8,128)(2,1)}, bf16[2464,256]{1,0:T(8,128)(2,1)S(1)}, u32[]{:S(2)}, u32[]{:S(2)}) %collective-permute-start.11) | collective-permute-done | bytes 1261600 | tf_op jit(solution)/shard_map/ppermute | solution.py:208
  88.2 2.5 %collective-permute-done.12.refs_5_ = bf16[2464,256]{1,0:T(8,128)(2,1)S(1)} collective-permute-done((bf16[2464,256]{1,0:T(8,128)(2,1)S(1)}, bf16[2464,256]{1,0:T(8,128)(2,1)S(1)}, u32[]{:S(2)}, u32[]{:S(2)}) %collective-permute-start.12) | collective-permute-done | bytes 1261600 | tf_op jit(solution)/shard_map/ppermute | solution.py:209
  91.8 35.8 %shard_map.105 = (f32[4,1232,256]{2,1,0:T(8,128)}, f32[4,1232,256]{2,1,0:T(8,128)}) custom-call(s32[4]{0:T(128)S(1)} %pad_add_fusion.order, bf16[1232,2464]{1,0:T(8,128)(2,1)} %bitcast.104, bf16[2464,256]{1,0:T(8,128)(2,1)S(1)} %bitcast.101, bf16[2464,256]{1,0:T(8,128)(2,1)} %collective-permute-done.5.refs_1_, bf16[2464,256]{1,0:T(8,128)(2,1)} %copy-done.1, ...), custom_call_target="tpu_custom_call" | custom-call | flops 1000 | bytes 1000 | tf_op jit(solution)/shard_map/pallas_call | solution.py:189
  127.5 4.4 %slice_bitcast_fusion = (f32[1232,256]{1,0:T(8,128)}, f32[1232,256]{1,0:T(8,128)S(1)}, f32[1232,256]{1,0:T(8,128)}, f32[1232,256]{1,0:T(8,128)}) fusion(f32[4,1232,256]{2,1,0:T(8,128)} %get-tuple-element.22), kind=kLoop, calls=%fused_computation.17 | loop fusion | bytes 10092544 | tf_op jit(solution)/shard_map/squeeze | solution.py:59
  132.6 2.8 %slice.66 = bf16[77,77,128]{2,1,0:T(8,128)(2,1)} slice(bf16[77,77,512]{2,1,0:T(8,128)(2,1)} %param.10), slice={[0:77], [0:77], [384:512]} | slice | bytes 3035648 | tf_op jit(solution)/shard_map/slice | solution.py:248
  135.4 3.5 %collective-permute-done.15 = f32[1232,256]{1,0:T(8,128)} collective-permute-done((f32[1232,256]{1,0:T(8,128)}, f32[1232,256]{1,0:T(8,128)}, u32[]{:S(2)}, u32[]{:S(2)}) %collective-permute-start.15) | collective-permute-done | bytes 1261600 | tf_op jit(solution)/shard_map/ppermute | solution.py:59
  138.9 3.8 %bitcast_add_fusion.1 = (f32[1232,256]{1,0:T(8,128)S(1)}, f32[1232,256]{1,0:T(8,128)S(1)}, f32[1232,256]{1,0:T(8,128)S(1)}) fusion(f32[1232,256]{1,0:T(8,128)} %collective-permute-done.18, f32[4,1232,256]{2,1,0:T(8,128)} %get-tuple-element.21, f32[1232,256]{1,0:T(8,128)} %collective-permute-done.15, f32[1232,256]{1,0:T(8,128)} %collective-permute-done.14), kind=kLoop, calls=%fused_computation.13 | loop fusion | flops 946176 | bytes 11354112 | tf_op jit(solution)/shard_map/add | solution.py:59
  142.8 4.2 %collective-permute-start.19 = (f32[616,256]{1,0:T(8,128)S(1)}, f32[616,256]{1,0:T(8,128)S(1)}, u32[]{:S(2)}, u32[]{:S(2)}) collective-permute-start(f32[616,256]{1,0:T(8,128)S(1)} %get-tuple-element.45), channel_id=1, source_target_pairs={{0,96},{16,112},{32,0},{48,16},{64,32},{80,48},{96,64},{112,80},{1... | collective-permute-start | bytes 1892360 | tf_op jit(solution)/shard_map/ppermute | solution.py:62
  146.9 5.1 %fusion.16 = f32[384,512,1]{1,0,2:T(8,128)S(1)} fusion(bf16[77,77,384]{2,1,0:T(8,128)(2,1)} %collective-permute-done, bf16[77,77,512]{2,1,0:T(8,128)(2,1)S(1)} %bitcast.103), kind=kOutput, calls=%fused_computation.59 | convolution fusion | flops 2331377664 | bytes 11411200 | tf_op jit(solution)/shard_map/dot_general | solution.py:241
  152.7 2.7 %collective-permute-start.2 = (f32[2,7,16,512]{3,2,1,0:T(8,128)S(1)}, f32[2,7,16,512]{3,2,1,0:T(8,128)}, u32[]{:S(2)}, u32[]{:S(2)}) collective-permute-start(f32[2,7,16,512]{3,2,1,0:T(8,128)S(1)} %bitcast.109), channel_id=1, source_target_pairs={{0,8},{2,10},{4,12},{6,14},{8,0},{10,2},{12,4},{14,6},{1,9},{3,11}... | collective-permute-start | bytes 1376264 | tf_op jit(solution)/shard_map/ppermute | solution.py:54
  155.5 5.2 %collective-permute-done.19 = f32[616,256]{1,0:T(8,128)S(1)} collective-permute-done((f32[616,256]{1,0:T(8,128)S(1)}, f32[616,256]{1,0:T(8,128)S(1)}, u32[]{:S(2)}, u32[]{:S(2)}) %collective-permute-start.19) | collective-permute-done | bytes 630816 | tf_op jit(solution)/shard_map/ppermute | solution.py:62
  163.5 5.8 %collective-permute-done.16 = f32[616,256]{1,0:T(8,128)S(1)} collective-permute-done((f32[616,256]{1,0:T(8,128)S(1)}, f32[616,256]{1,0:T(8,128)S(1)}, u32[]{:S(2)}, u32[]{:S(2)}) %collective-permute-start.16) | collective-permute-done | bytes 630816 | tf_op jit(solution)/shard_map/ppermute | solution.py:61
  170.5 5.2 %collective-permute-done.1 = f32[2,7,16,512]{3,2,1,0:T(8,128)S(1)} collective-permute-done((f32[2,7,16,512]{3,2,1,0:T(8,128)S(1)}, f32[2,7,16,512]{3,2,1,0:T(8,128)S(1)}, u32[]{:S(2)}, u32[]{:S(2)}) %collective-permute-start.1) | collective-permute-done | bytes 458784 | tf_op jit(solution)/shard_map/ppermute | solution.py:54
  180.7 5.5 %collective-permute-done.4 = f32[7,16,512]{2,1,0:T(8,128)S(1)} collective-permute-done((f32[7,16,512]{2,1,0:T(8,128)S(1)}, f32[7,16,512]{2,1,0:T(8,128)S(1)}, u32[]{:S(2)}, u32[]{:S(2)}) %collective-permute-start.4) | collective-permute-done | bytes 229408 | tf_op jit(solution)/shard_map/ppermute | solution.py:71
  186.9 11.3 %collective-permute-done.20.refs_2_ = f32[1232,256]{1,0:T(8,128)S(1)} collective-permute-done((f32[1232,256]{1,0:T(8,128)}, f32[1232,256]{1,0:T(8,128)S(1)}, u32[]{:S(2)}, u32[]{:S(2)}) %collective-permute-start.20) | collective-permute-done | bytes 1261600 | tf_op jit(solution)/shard_map/ppermute | solution.py:66
  198.2 3.4 %collective-permute-done.17.refs_1_ = f32[1232,256]{1,0:T(8,128)} collective-permute-done((f32[1232,256]{1,0:T(8,128)}, f32[1232,256]{1,0:T(8,128)}, u32[]{:S(2)}, u32[]{:S(2)}) %collective-permute-start.17) | collective-permute-done | bytes 1261600 | tf_op jit(solution)/shard_map/ppermute | solution.py:65
  201.6 5.0 %fusion.17 = f32[128,512,1]{1,0,2:T(8,128)} fusion(bf16[77,77,128]{2,1,0:T(8,128)(2,1)} %collective-permute-done.6, bf16[77,77,512]{2,1,0:T(8,128)(2,1)} %src.1), kind=kOutput, calls=%fused_computation.60 | convolution fusion | flops 777125888 | bytes 7851264 | tf_op jit(solution)/shard_map/dot_general | solution.py:241
  208.5 2.8 %collective-permute-start.22 = (f32[2,1,16,512]{3,2,1,0:T(8,128)}, f32[2,1,16,512]{3,2,1,0:T(8,128)S(1)}, u32[]{:S(2)}, u32[]{:S(2)}) collective-permute-start(f32[2,1,16,512]{3,2,1,0:T(8,128)} %get-tuple-element.29), channel_id=1, source_target_pairs={{0,8},{2,10},{4,12},{6,14},{8,0},{10,2},{12,4},{14,6},{1,9},{3,11}... | collective-permute-start | bytes 196616 | tf_op jit(solution)/shard_map/ppermute | solution.py:102
  211.8 3.0 %collective-permute-done.21 = f32[2,1,16,512]{3,2,1,0:T(8,128)S(1)} collective-permute-done((f32[2,1,16,512]{3,2,1,0:T(8,128)}, f32[2,1,16,512]{3,2,1,0:T(8,128)S(1)}, u32[]{:S(2)}, u32[]{:S(2)}) %collective-permute-start.21) | collective-permute-done | bytes 65568 | tf_op jit(solution)/shard_map/ppermute | solution.py:102
  218.3 3.8 %collective-permute-done.24 = f32[1,16,512]{2,1,0:T(8,128)S(1)} collective-permute-done((f32[1,16,512]{2,1,0:T(8,128)S(1)}, f32[1,16,512]{2,1,0:T(8,128)S(1)}, u32[]{:S(2)}, u32[]{:S(2)}) %collective-permute-start.24) | collective-permute-done | bytes 32800 | tf_op jit(solution)/shard_map/ppermute | solution.py:71
  222.4 2.5 %fusion.1 = f32[1232,256]{1,0:T(8,128)S(1)} fusion(f32[1232,256]{1,0:T(8,128)S(1)} %copy-done.6, f32[1232,256]{1,0:T(8,128)} %collective-permute-done.17.refs_1_, f32[1232,256]{1,0:T(8,128)} %collective-permute-done.29, f32[4,1232,256]{2,1,0:T(8,128)} %get-tuple-element.21), kind=kLoop, calls=%fused_computation.12 | loop fusion | flops 946176 | bytes 6307840 | tf_op jit(solution)/shard_map/add | solution.py:67
  226.0 2.5 %collective-permute-start.28 = (f32[16,512]{1,0:T(8,128)S(1)}, f32[16,512]{1,0:T(8,128)S(1)}, u32[]{:S(2)}, u32[]{:S(2)}) collective-permute-start(f32[16,512]{1,0:T(8,128)S(1)} %get-tuple-element.50), channel_id=1, source_target_pairs={{0,96},{16,112},{32,0},{48,16},{64,32},{80,48},{96,64},{112,80},{1... | collective-permute-start | bytes 98312 | tf_op jit(solution)/shard_map/ppermute | solution.py:54
  (114 shorter events, 31.9 us)
Async XLA Ops:
  5.7 126.2 %collective-permute-start = (bf16[77,77,384]{2,1,0:T(8,128)(2,1)}, bf16[77,77,384]{2,1,0:T(8,128)(2,1)}, u32[]{:S(2)}, u32[]{:S(2)}) collective-permute-start(bf16[77,77,384]{2,1,0:T(8,128)(2,1)} %slice.65), channel_id=1, source_target_pairs={{0,1},{1,0},{2,3},{3,2},{4,5},{5,4},{6,7},{7,6},{8,9},{9,8},{10,11... | collective-permute-start | bytes 13660424 | tf_op jit(solution)/shard_map/ppermute | solution.py:238
  7.4 29.5 %collective-permute-start.7 = (bf16[2464,256]{1,0:T(8,128)(2,1)S(1)}, bf16[2464,256]{1,0:T(8,128)(2,1)S(1)}, u32[]{:S(2)}, u32[]{:S(2)}) collective-permute-start(bf16[2464,256]{1,0:T(8,128)(2,1)S(1)} %bitcast.98), channel_id=1, source_target_pairs={{0,12},{2,14},{4,0},{6,2},{8,4},{10,6},{12,8},{14,10},{1,13},{3,15... | collective-permute-start | bytes 3784712 | tf_op jit(solution)/shard_map/ppermute | solution.py:202
  10.1 31.4 %collective-permute-start.8 = (bf16[2464,256]{1,0:T(8,128)(2,1)S(1)}, bf16[2464,256]{1,0:T(8,128)(2,1)}, u32[]{:S(2)}, u32[]{:S(2)}) collective-permute-start(bf16[2464,256]{1,0:T(8,128)(2,1)S(1)} %bitcast.99), channel_id=1, source_target_pairs={{0,4},{2,6},{4,8},{6,10},{8,12},{10,14},{12,0},{14,2},{1,5},{3,7},... | collective-permute-start | bytes 3784712 | tf_op jit(solution)/shard_map/ppermute | solution.py:201
  10.1 33.4 %collective-permute-start.5 = (bf16[2464,256]{1,0:T(8,128)(2,1)S(1)}, bf16[2464,256]{1,0:T(8,128)(2,1)}, u32[]{:S(2)}, u32[]{:S(2)}) collective-permute-start(bf16[2464,256]{1,0:T(8,128)(2,1)S(1)} %bitcast.100), channel_id=1, source_target_pairs={{0,3},{1,2},{2,1},{3,0},{4,7},{5,6},{6,5},{7,4},{8,11},{9,10},{10,... | collective-permute-start | bytes 3784712 | tf_op jit(solution)/shard_map/ppermute | solution.py:200
  37.9 16.4 %collective-permute-start.10 = (bf16[1232,256]{1,0:T(8,128)(2,1)}, bf16[1232,256]{1,0:T(8,128)(2,1)S(1)}, u32[]{:S(2)}, u32[]{:S(2)}) collective-permute-start(bf16[1232,256]{1,0:T(8,128)(2,1)} %slice.69), channel_id=1, source_target_pairs={{0,12},{2,14},{4,0},{6,2},{8,4},{10,6},{12,8},{14,10},{1,13},{3,15... | collective-permute-start | bytes 1892360 | tf_op jit(solution)/shard_map/ppermute | solution.py:204
  43.5 16.1 %collective-permute-start.9 = (bf16[1232,256]{1,0:T(8,128)(2,1)}, bf16[1232,256]{1,0:T(8,128)(2,1)}, u32[]{:S(2)}, u32[]{:S(2)}) collective-permute-start(bf16[1232,256]{1,0:T(8,128)(2,1)} %slice.68), channel_id=1, source_target_pairs={{0,4},{2,6},{4,8},{6,10},{8,12},{10,14},{12,0},{14,2},{1,5},{3,7},... | collective-permute-start | bytes 1892360 | tf_op jit(solution)/shard_map/ppermute | solution.py:203
  59.6 27.4 %collective-permute-start.11 = (bf16[2464,256]{1,0:T(8,128)(2,1)}, bf16[2464,256]{1,0:T(8,128)(2,1)S(1)}, u32[]{:S(2)}, u32[]{:S(2)}) collective-permute-start(bf16[2464,256]{1,0:T(8,128)(2,1)} %collective-permute-done.5.refs_1_), channel_id=1, source_target_pairs={{0,12},{2,14},{4,0},{6,2},{8,4},{10,6},{12,8},{14,10},{1,13},{3,15... | collective-permute-start | bytes 3784712 | tf_op jit(solution)/shard_map/ppermute | solution.py:208
  59.6 28.6 %collective-permute-start.13 = (bf16[2464,256]{1,0:T(8,128)(2,1)}, bf16[2464,256]{1,0:T(8,128)(2,1)S(1)}, u32[]{:S(2)}, u32[]{:S(2)}) collective-permute-start(bf16[2464,256]{1,0:T(8,128)(2,1)} %collective-permute-done.5.refs_1_), channel_id=1, source_target_pairs={{0,4},{2,6},{4,8},{6,10},{8,12},{10,14},{12,0},{14,2},{1,5},{3,7},... | collective-permute-start | bytes 3784712 | tf_op jit(solution)/shard_map/ppermute | solution.py:207
  62.8 27.9 %collective-permute-start.12 = (bf16[2464,256]{1,0:T(8,128)(2,1)S(1)}, bf16[2464,256]{1,0:T(8,128)(2,1)S(1)}, u32[]{:S(2)}, u32[]{:S(2)}) collective-permute-start(bf16[2464,256]{1,0:T(8,128)(2,1)S(1)} %constant_dynamic-update-slice_fusion.refs_4_), channel_id=1, source_target_pairs={{0,3},{1,2},{2,1},{3,0},{4,7},{5,6},{6,5},{7,4},{8,11},{9,10},{10,... | collective-permute-start | bytes 3784712 | tf_op jit(solution)/shard_map/ppermute | solution.py:209
  132.0 3.4 %collective-permute-start.14 = (f32[1232,256]{1,0:T(8,128)}, f32[1232,256]{1,0:T(8,128)}, u32[]{:S(2)}, u32[]{:S(2)}) collective-permute-start(f32[1232,256]{1,0:T(8,128)} %get-tuple-element.23), channel_id=1, source_target_pairs={{0,16},{16,0},{32,48},{48,32},{64,80},{80,64},{96,112},{112,96},{1... | collective-permute-start | bytes 3784712 | tf_op jit(solution)/shard_map/ppermute | solution.py:59
  132.0 6.9 %collective-permute-start.15 = (f32[1232,256]{1,0:T(8,128)}, f32[1232,256]{1,0:T(8,128)}, u32[]{:S(2)}, u32[]{:S(2)}) collective-permute-start(f32[1232,256]{1,0:T(8,128)} %get-tuple-element.24), channel_id=1, source_target_pairs={{0,16},{16,0},{32,48},{48,32},{64,80},{80,64},{96,112},{112,96},{1... | collective-permute-start | bytes 3784712 | tf_op jit(solution)/shard_map/ppermute | solution.py:59
  132.5 6.4 %collective-permute-start.18 = (f32[1232,256]{1,0:T(8,128)S(1)}, f32[1232,256]{1,0:T(8,128)}, u32[]{:S(2)}, u32[]{:S(2)}) collective-permute-start(f32[1232,256]{1,0:T(8,128)S(1)} %get-tuple-element.25), channel_id=1, source_target_pairs={{0,16},{16,0},{32,48},{48,32},{64,80},{80,64},{96,112},{112,96},{1... | collective-permute-start | bytes 3784712 | tf_op jit(solution)/shard_map/ppermute | solution.py:59
  135.4 51.5 %collective-permute-start.6 = (bf16[77,77,128]{2,1,0:T(8,128)(2,1)}, bf16[77,77,128]{2,1,0:T(8,128)(2,1)}, u32[]{:S(2)}, u32[]{:S(2)}) collective-permute-start(bf16[77,77,128]{2,1,0:T(8,128)(2,1)} %slice.66), channel_id=1, source_target_pairs={{0,1},{1,0},{2,3},{3,2},{4,5},{5,4},{6,7},{7,6},{8,9},{9,8},{10,11... | collective-permute-start | bytes 4553480 | tf_op jit(solution)/shard_map/ppermute | solution.py:249
  142.8 17.9 %collective-permute-start.19 = (f32[616,256]{1,0:T(8,128)S(1)}, f32[616,256]{1,0:T(8,128)S(1)}, u32[]{:S(2)}, u32[]{:S(2)}) collective-permute-start(f32[616,256]{1,0:T(8,128)S(1)} %get-tuple-element.45), channel_id=1, source_target_pairs={{0,96},{16,112},{32,0},{48,16},{64,32},{80,48},{96,64},{112,80},{1... | collective-permute-start | bytes 1892360 | tf_op jit(solution)/shard_map/ppermute | solution.py:62
  152.0 17.2 %collective-permute-start.16 = (f32[616,256]{1,0:T(8,128)S(1)}, f32[616,256]{1,0:T(8,128)S(1)}, u32[]{:S(2)}, u32[]{:S(2)}) collective-permute-start(f32[616,256]{1,0:T(8,128)S(1)} %get-tuple-element.46), channel_id=1, source_target_pairs={{0,32},{16,48},{32,64},{48,80},{64,96},{80,112},{96,0},{112,16},{1... | collective-permute-start | bytes 1892360 | tf_op jit(solution)/shard_map/ppermute | solution.py:61
  152.3 23.4 %collective-permute-start.1 = (f32[2,7,16,512]{3,2,1,0:T(8,128)S(1)}, f32[2,7,16,512]{3,2,1,0:T(8,128)S(1)}, u32[]{:S(2)}, u32[]{:S(2)}) collective-permute-start(f32[2,7,16,512]{3,2,1,0:T(8,128)S(1)} %bitcast.111), channel_id=1, source_target_pairs={{0,4},{2,6},{4,8},{6,10},{8,12},{10,14},{12,0},{14,2},{1,5},{3,7},... | collective-permute-start | bytes 1376264 | tf_op jit(solution)/shard_map/ppermute | solution.py:54
  152.7 23.8 %collective-permute-start.2 = (f32[2,7,16,512]{3,2,1,0:T(8,128)S(1)}, f32[2,7,16,512]{3,2,1,0:T(8,128)}, u32[]{:S(2)}, u32[]{:S(2)}) collective-permute-start(f32[2,7,16,512]{3,2,1,0:T(8,128)S(1)} %bitcast.109), channel_id=1, source_target_pairs={{0,8},{2,10},{4,12},{6,14},{8,0},{10,2},{12,4},{14,6},{1,9},{3,11}... | collective-permute-start | bytes 1376264 | tf_op jit(solution)/shard_map/ppermute | solution.py:54
  160.7 15.9 %collective-permute-start.3 = (f32[2,7,16,512]{3,2,1,0:T(8,128)S(1)}, f32[2,7,16,512]{3,2,1,0:T(8,128)}, u32[]{:S(2)}, u32[]{:S(2)}) collective-permute-start(f32[2,7,16,512]{3,2,1,0:T(8,128)S(1)} %bitcast.110), channel_id=1, source_target_pairs={{0,12},{2,14},{4,0},{6,2},{8,4},{10,6},{12,8},{14,10},{1,13},{3,15... | collective-permute-start | bytes 1376264 | tf_op jit(solution)/shard_map/ppermute | solution.py:54
  169.3 28.9 %collective-permute-start.20 = (f32[1232,256]{1,0:T(8,128)}, f32[1232,256]{1,0:T(8,128)S(1)}, u32[]{:S(2)}, u32[]{:S(2)}) collective-permute-start(f32[1232,256]{1,0:T(8,128)} %pad_maximum_fusion.1), channel_id=1, source_target_pairs={{0,96},{16,112},{32,0},{48,16},{64,32},{80,48},{96,64},{112,80},{1... | collective-permute-start | bytes 3784712 | tf_op jit(solution)/shard_map/ppermute | solution.py:66
  176.5 25.0 %collective-permute-start.17 = (f32[1232,256]{1,0:T(8,128)}, f32[1232,256]{1,0:T(8,128)}, u32[]{:S(2)}, u32[]{:S(2)}) collective-permute-start(f32[1232,256]{1,0:T(8,128)} %pad_maximum_fusion), channel_id=1, source_target_pairs={{0,32},{16,48},{32,64},{48,80},{64,96},{80,112},{96,0},{112,16},{1... | collective-permute-start | bytes 3784712 | tf_op jit(solution)/shard_map/ppermute | solution.py:65
  178.2 7.9 %collective-permute-start.4 = (f32[7,16,512]{2,1,0:T(8,128)S(1)}, f32[7,16,512]{2,1,0:T(8,128)S(1)}, u32[]{:S(2)}, u32[]{:S(2)}) collective-permute-start(f32[7,16,512]{2,1,0:T(8,128)S(1)} %dynamic-slice_bitcast_fusion), channel_id=1, source_target_pairs={{0,2},{2,0},{4,6},{6,4},{8,10},{10,8},{12,14},{14,12},{1,3},{3,1},... | collective-permute-start | bytes 688136 | tf_op jit(solution)/shard_map/ppermute | solution.py:71
  180.6 41.8 %collective-permute-start.29 = (f32[1232,256]{1,0:T(8,128)S(1)}, f32[1232,256]{1,0:T(8,128)}, u32[]{:S(2)}, u32[]{:S(2)}) collective-permute-start(f32[1232,256]{1,0:T(8,128)S(1)} %copy-done.4), channel_id=1, source_target_pairs={{0,16},{16,0},{32,48},{48,32},{64,80},{80,64},{96,112},{112,96},{1... | collective-permute-start | bytes 3784712 | tf_op jit(solution)/shard_map/ppermute | solution.py:59
  206.6 15.5 %slice-start.2 = ((f32[7,16,512]{2,1,0:T(8,128)}), f32[4,16,512]{2,1,0:T(8,128)S(1)}, s32[]{:S(2)}) async-start(f32[7,16,512]{2,1,0:T(8,128)} %bitcast_add_fusion.4.refs_0_), calls=%async_computation.2 | async-start | bytes 262144 | tf_op jit(solution)/shard_map/slice | solution.py:259
  206.6 15.5 %slice-start.3 = ((f32[7,16,512]{2,1,0:T(8,128)}), f32[3,16,512]{2,1,0:T(8,128)S(1)}, s32[]{:S(2)}) async-start(f32[7,16,512]{2,1,0:T(8,128)} %bitcast_add_fusion.4.refs_0_), calls=%async_computation.3 | async-start | bytes 196608 | tf_op jit(solution)/shard_map/slice | solution.py:259
  208.4 6.4 %collective-permute-start.21 = (f32[2,1,16,512]{3,2,1,0:T(8,128)}, f32[2,1,16,512]{3,2,1,0:T(8,128)S(1)}, u32[]{:S(2)}, u32[]{:S(2)}) collective-permute-start(f32[2,1,16,512]{3,2,1,0:T(8,128)} %get-tuple-element.28), channel_id=1, source_target_pairs={{0,4},{2,6},{4,8},{6,10},{8,12},{10,14},{12,0},{14,2},{1,5},{3,7},... | collective-permute-start | bytes 196616 | tf_op jit(solution)/shard_map/ppermute | solution.py:102
  208.5 6.2 %collective-permute-start.22 = (f32[2,1,16,512]{3,2,1,0:T(8,128)}, f32[2,1,16,512]{3,2,1,0:T(8,128)S(1)}, u32[]{:S(2)}, u32[]{:S(2)}) collective-permute-start(f32[2,1,16,512]{3,2,1,0:T(8,128)} %get-tuple-element.29), channel_id=1, source_target_pairs={{0,8},{2,10},{4,12},{6,14},{8,0},{10,2},{12,4},{14,6},{1,9},{3,11}... | collective-permute-start | bytes 196616 | tf_op jit(solution)/shard_map/ppermute | solution.py:102
  211.3 4.5 %collective-permute-start.23 = (f32[2,1,16,512]{3,2,1,0:T(8,128)}, f32[2,1,16,512]{3,2,1,0:T(8,128)S(1)}, u32[]{:S(2)}, u32[]{:S(2)}) collective-permute-start(f32[2,1,16,512]{3,2,1,0:T(8,128)} %get-tuple-element.30), channel_id=1, source_target_pairs={{0,12},{2,14},{4,0},{6,2},{8,4},{10,6},{12,8},{14,10},{1,13},{3,15... | collective-permute-start | bytes 196616 | tf_op jit(solution)/shard_map/ppermute | solution.py:102
  216.6 5.5 %collective-permute-start.24 = (f32[1,16,512]{2,1,0:T(8,128)S(1)}, f32[1,16,512]{2,1,0:T(8,128)S(1)}, u32[]{:S(2)}, u32[]{:S(2)}) collective-permute-start(f32[1,16,512]{2,1,0:T(8,128)S(1)} %dynamic-slice_bitcast_fusion.5), channel_id=1, source_target_pairs={{0,2},{2,0},{4,6},{6,4},{8,10},{10,8},{12,14},{14,12},{1,3},{3,1},... | collective-permute-start | bytes 98312 | tf_op jit(solution)/shard_map/ppermute | solution.py:71
  222.2 2.6 %collective-permute-start.25 = (f32[4,16,512]{2,1,0:T(8,128)S(1)}, f32[4,16,512]{2,1,0:T(8,128)S(1)}, u32[]{:S(2)}, u32[]{:S(2)}) collective-permute-start(f32[4,16,512]{2,1,0:T(8,128)S(1)} %dynamic-slice_bitcast_fusion.1), channel_id=1, source_target_pairs={{0,16},{16,0},{32,48},{48,32},{64,80},{80,64},{96,112},{112,96},{1... | collective-permute-start | bytes 393224 | tf_op jit(solution)/shard_map/ppermute | solution.py:71
  224.9 5.5 %collective-permute-start.26 = (f32[16,512]{1,0:T(8,128)S(1)}, f32[16,512]{1,0:T(8,128)S(1)}, u32[]{:S(2)}, u32[]{:S(2)}) collective-permute-start(f32[16,512]{1,0:T(8,128)S(1)} %get-tuple-element.49), channel_id=1, source_target_pairs={{0,32},{16,48},{32,64},{48,80},{64,96},{80,112},{96,0},{112,16},{1... | collective-permute-start | bytes 98312 | tf_op jit(solution)/shard_map/ppermute | solution.py:54
  225.5 5.4 %collective-permute-start.27 = (f32[16,512]{1,0:T(8,128)S(1)}, f32[16,512]{1,0:T(8,128)S(1)}, u32[]{:S(2)}, u32[]{:S(2)}) collective-permute-start(f32[16,512]{1,0:T(8,128)S(1)} %get-tuple-element.51), channel_id=1, source_target_pairs={{0,64},{16,80},{32,96},{48,112},{64,0},{80,16},{96,32},{112,48},{1... | collective-permute-start | bytes 98312 | tf_op jit(solution)/shard_map/ppermute | solution.py:54
  226.0 5.3 %collective-permute-start.28 = (f32[16,512]{1,0:T(8,128)S(1)}, f32[16,512]{1,0:T(8,128)S(1)}, u32[]{:S(2)}, u32[]{:S(2)}) collective-permute-start(f32[16,512]{1,0:T(8,128)S(1)} %get-tuple-element.50), channel_id=1, source_target_pairs={{0,96},{16,112},{32,0},{48,16},{64,32},{80,48},{96,64},{112,80},{1... | collective-permute-start | bytes 98312 | tf_op jit(solution)/shard_map/ppermute | solution.py:54
  (18 other events, 121.2 us)

commit v3 on v2

--- a/solution.py
+++ b/solution.py
@@ -55,16 +55,16 @@
     return kept + got[0] + got[1] + got[2]
 
 
-def ring_row(keep, send, gate):
-    got = {r: keep[r] + lax.ppermute(after(send[r], gate), "row", SWAP_CORE) for r in (2, 1, 3, 0)}
-    half = keep.shape[1] // 2
-    up = lax.ppermute(got[2][:half], "row", shift_z(1))
-    down = lax.ppermute(got[2][half:], "row", shift_z(3))
-    right = jnp.concatenate([got[1][:half] + up, got[1][half:]], axis=0)
-    left = jnp.concatenate([got[3][:half], got[3][half:] + down], axis=0)
-    below = lax.ppermute(right, "row", shift_z(1))
-    above = lax.ppermute(left, "row", shift_z(3))
-    return got[0] + below + above, (below, above)
+def swap_add(keep, send):
+    return [a + lax.ppermute(b, "row", SWAP_CORE) for a, b in zip(keep, send)]
+
+
+def up_z(value):
+    return lax.ppermute(value, "row", shift_z(1))
+
+
+def down_z(value):
+    return lax.ppermute(value, "row", shift_z(3))
 
 
 def two_way(blocks, mine, axis_name, swap):
@@ -72,14 +72,14 @@
 
 
 def turn_kernel(start, src, *refs):
-    dst = refs[-src.shape[0] :]
+    dst = refs[-src.shape[1] :]
     for s, d in enumerate(dst):
-        d[...] = src[(start[0] + s) % len(dst)]
-
-
-def turn(blocks, start, gates):
-    n = blocks.shape[0]
-    one = jax.ShapeDtypeStruct(blocks.shape[1:], blocks.dtype)
+        d[...] = src[:, (start[0] + s) % len(dst)]
+
+
+def turn(blocks, start, gates, cost):
+    n = blocks.shape[1]
+    one = jax.ShapeDtypeStruct(blocks.shape[:1] + blocks.shape[2:], blocks.dtype)
     return pl.pallas_call(
         turn_kernel,
         in_specs=[
@@ -89,21 +89,17 @@
         + [pl.BlockSpec(memory_space=pl.ANY)] * len(gates),
         out_specs=[pl.BlockSpec(memory_space=pltpu.VMEM)] * n,
         out_shape=[one] * n,
-        cost_estimate=LONG,
+        cost_estimate=cost,
     )(start.reshape(1).astype(jnp.int32), blocks, *gates)
 
 
-def reduce_col(part, x, hi, gates=()):
+def reduce_col(part, x, hi, gates, cost):
     n, rows, pair_occ = part.shape
     keep = rows // (NX * NHI)
-    v = part.reshape(n, NX, NHI, keep, pair_occ).transpose(1, 2, 0, 3, 4)
-    if gates:
-        kept, *sent = turn(v, x, gates)
-        got = [lax.ppermute(b, "col", shift_x(s + 1)) for s, b in enumerate(sent)]
-        v = kept + got[0] + got[1] + got[2]
-    else:
-        v = four_way(v, x, "col", shift_x)
-    return two_way(v, hi, "col", SWAP_HI)
+    kept, *sent = turn(part.reshape(n, NX, NHI, keep, pair_occ), x, gates, cost)
+    got = [lax.ppermute(b, "col", shift_x(s + 1)) for s, b in enumerate(sent)]
+    v = kept + got[0] + got[1] + got[2]
+    return pick(v, hi, 1) + lax.ppermute(pick(v, 1 - hi, 1), "col", SWAP_HI)
 
 
 def amp_kernel(src, dst, rows_in, rows_out):
@@ -153,46 +149,81 @@
     return out.reshape(virt_col * occ_dev, virt_row * OCC)
 
 
-def cycle_kernel(order, amp, *refs, blocks_in):
-    blocks, (keep, send) = refs[:blocks_in], refs[-NCORE:]
-    step = pl.program_id(0)
-    swapped = order[1] != order[2]
-    for s in range(NX):
-
-        @pl.when(step == s)
-        def _():
-            for i in range(NHI):
-                r = jnp.dot(amp[...], blocks[NHI * s + i][...], preferred_element_type=F32)
-
-                @pl.when(swapped)
+def cycle_kernel(order, amp, *refs, chips, blocks_in):
+    count = NCORE * len(chips)
+    blocks, outs = refs[:blocks_in], refs[-2 * count - 6 : -6]
+    amp_buf, buf, res, amp_sems, sems, out_sems = refs[-6:]
+    x, hi, core, z = order[0], order[1], order[2], order[3]
+    swapped = hi != core
+    half = amp.shape[0] // 2
+    amp_in = [
+        pltpu.make_async_copy(amp.at[pl.ds(i * half, half)], amp_buf.at[pl.ds(i * half, half)], amp_sems.at[i])
+        for i in range(2)
+    ]
+    amp_in[0].start()
+    copies = []
+    width = buf.shape[2] // NCORE
+    for n, r in enumerate(chips):
+        s = (z + r + NX - x) % NX
+        for other in range(NCORE):
+            columns = buf.at[n, :, pl.ds(other * width, width)]
+            copies.append(pltpu.make_async_copy(blocks[0], columns, sems.at[n, other]))
+            for k in range(blocks_in):
+                block, near = divmod(k, NHI)
+                here = (s == block) & (swapped == bool(near ^ other))
+
+                @pl.when(here)
                 def _():
-                    (send, keep)[i][...] = r
-
-                @pl.when(jnp.logical_not(swapped))
-                def _():
-                    (keep, send)[i][...] = r
-
-
-def cycle_dot(order, amp, blocks, gates):
+                    pltpu.make_async_copy(blocks[k], columns, sems.at[n, other]).start()
+
+        if n == 0:
+            amp_in[1].start()
+
+    writes = {}
+    for n in range(len(chips)):
+        for copy in copies[NCORE * n : NCORE * (n + 1)]:
+            copy.wait()
+        for i in range(2):
+            if n == 0:
+                amp_in[i].wait()
+            else:
+                for write in writes[n - 1, i]:
+                    write.wait()
+            res[i] = jnp.dot(amp_buf[i * half : (i + 1) * half], buf[n], preferred_element_type=F32)
+            writes[n, i] = [
+                pltpu.make_async_copy(
+                    res.at[i, :, pl.ds(other * width, width)], outs[2 * (NCORE * n + other) + i], out_sems.at[i, other]
+                )
+                for other in range(NCORE)
+            ]
+            for write in writes[n, i]:
+                write.start()
+    for i in range(2):
+        for write in writes[len(chips) - 1, i]:
+            write.wait()
+
+
+def cycle_dot(order, amp, blocks, chips, gates):
     m, k = amp.shape
     n = blocks[0].shape[1]
-    whole = lambda s, o: (0, 0)
-    once = pl.Buffered(1)
-    grid_spec = pltpu.PrefetchScalarGridSpec(
-        num_scalar_prefetch=1,
-        grid=(NX,),
-        in_specs=[pl.BlockSpec((m, k), whole, pipeline_mode=once)]
-        + [pl.BlockSpec((k, n), whole, pipeline_mode=once) for _ in blocks]
-        + [pl.BlockSpec(memory_space=pl.ANY) for _ in gates],
-        out_specs=[pl.BlockSpec((pl.Squeezed(), m, n), lambda s, o: ((o[0] + s + NZ - o[3]) % NZ, 0, 0))] * NCORE,
-    )
-    return pl.pallas_call(
-        functools.partial(cycle_kernel, blocks_in=len(blocks)),
-        grid_spec=grid_spec,
-        out_shape=[jax.ShapeDtypeStruct((NZ, m, n), F32)] * NCORE,
+    count = NCORE * len(chips)
+    out = pl.pallas_call(
+        functools.partial(cycle_kernel, chips=chips, blocks_in=len(blocks)),
+        in_specs=[pl.BlockSpec(memory_space=pltpu.SMEM)] + [pl.BlockSpec(memory_space=pl.ANY)] * (1 + len(blocks) + len(gates)),
+        out_specs=[pl.BlockSpec(memory_space=pl.ANY)] * (2 * count),
+        out_shape=[jax.ShapeDtypeStruct((m // 2, n), F32)] * (2 * count),
+        scratch_shapes=[
+            pltpu.VMEM((m, k), amp.dtype),
+            pltpu.VMEM((len(chips), k, NCORE * n), amp.dtype),
+            pltpu.VMEM((2, m // 2, NCORE * n), F32),
+            pltpu.SemaphoreType.DMA((2,)),
+            pltpu.SemaphoreType.DMA((len(chips), NCORE)),
+            pltpu.SemaphoreType.DMA((2, NCORE)),
+        ],
         compiler_params=pltpu.CompilerParams(vmem_limit_bytes=50 << 20),
         cost_estimate=SMALL,
     )(order, amp, *blocks, *gates)
+    return {r: (out[4 * i : 4 * i + 2], out[4 * i + 2 : 4 * i + 4]) for i, r in enumerate(chips)}
 
 
 def gather_cycle(own, gate):
@@ -232,7 +263,7 @@
     x, hi = col // NHI, col % NHI
 
     chunks = ladder_ints.shape[2] // LANES
-    begun = chunks - 1
+    begun = chunks // 2
     cut = begun * LANES
     most = lax.slice_in_dim(ladder_ints, 0, cut, axis=2)
     got_most = lax.ppermute(most, "depth", SWAP_DEPTH)
@@ -248,14 +279,20 @@
     last = lax.slice_in_dim(after(ladder_ints, blocks[1]), cut, chunks * LANES, axis=2)
     got_last = lax.ppermute(last, "depth", SWAP_DEPTH)
     order = jnp.stack([x, hi, core, z]).astype(jnp.int32)
-    keep, send = cycle_dot(order, cycle_amp, blocks, (own_dot,))
-    cycle_sum, cycle_parts = ring_row(keep, send, got_most)
+    parts = cycle_dot(order, cycle_amp, blocks, (2, 1, 3, 0), (own_dot, got_most))
+    far = swap_add(*parts[2])
+    up, down = up_z(far[0]), down_z(far[1])
+    right, left = swap_add(*parts[1]), swap_add(*parts[3])
+    right_rest, left_rest = up_z(right[1]), down_z(left[0])
+    below, above = up_z(right[0] + up), down_z(left[1] + down)
+    mine = swap_add(*parts[0])
+    cycle_sum = jnp.concatenate([mine[0] + below + left_rest, mine[1] + right_rest + above], axis=0)
     cycle_sum = cycle_sum.reshape(virt_col, occ_dev, cycle_ints.shape[2])
 
-    most_part = ladder_dot(after(got_most, corner(keep))).reshape(begun, LANES, pair_occ)
-    last_part = ladder_dot(after(got_last, *cycle_parts)).reshape(chunks - begun, LANES, pair_occ)
-    early = reduce_col(jnp.concatenate([own_part, most_part], axis=0), x, hi)
-    late = reduce_col(last_part, x, hi, gates=(early, *cycle_parts))
+    most_part = ladder_dot(got_most).reshape(begun, LANES, pair_occ)
+    last_part = ladder_dot(got_last).reshape(chunks - begun, LANES, pair_occ)
+    early = reduce_col(jnp.concatenate([own_part, most_part], axis=0), x, hi, (up, down, right[1], left[0]), SMALL)
+    late = reduce_col(last_part, x, hi, (early, below, above, right_rest, left_rest), LONG)
     ladder_mine, rest = early[:chunks], jnp.concatenate([early[chunks:], late], axis=0)
     both = jnp.where(depth == 0, jnp.concatenate([ladder_mine, rest], 0), jnp.concatenate([rest, ladder_mine], 0))
     v = both.reshape(NZ, NCORE, both.shape[1], pair_occ).transpose(1, 0, 2, 3)

time: 233 us -> 203 us (0.87)
  waiting for transfers between devices: 90.6 us -> 62.4 us
  starting transfers between devices: 33.8 us -> 46.8 us
  Pallas kernels: 54.7 us -> 43.4 us
  local copies, waits for them, and re-layouts: 19.6 us -> 15.6 us
    ppermute x1, waiting for transfers between devices: 0.01 us -> 16.9 us  [body(): got_most = lax.ppermute(most, 'depth', SWAP_DEPTH)]
    ppermute x8 -> x16, waiting for transfers between devices: 29.2 us -> 14.6 us  [the longest x3 11.7 us: up_z(): return lax.ppermute(value, 'row', shift_z(1))]
    pallas_call x1, Pallas kernels: 35.8 us -> 21.6 us  [cycle_dot(): pl.pallas_call(functools.partial(cycle_kernel, chips=chips, blocks_in=len...]
    ppermute x1, waiting for transfers between devices: 14.2 us -> 0.01 us  [gather_cycle(): across_r = lax.ppermute(again, 'col', shift_x(-1))]
    ppermute x3 -> x6, waiting for transfers between devices: 3.99 us -> 16.3 us  [reduce_col(): got = [lax.ppermute(b, 'col', shift_x(s + 1)) for s, b in enumerate(sent)]]
    ppermute x8 -> x16, starting transfers between devices: 4.91 us -> 16.8 us  [the longest x3 8.17 us: down_z(): return lax.ppermute(value, 'row', shift_z(3))]
    ppermute x1, waiting for transfers between devices: 10.7 us -> 0.46 us  [gather_cycle(): far_b = lax.ppermute(after(own_r, gate)[half:], 'col', shift_x(-1))]
    ppermute x3 -> x1, waiting for transfers between devices: 9.3 us -> 1.24 us  [two_way(): lax.ppermute(pick(blocks, 1 - mine, 0), axis_name, swap)]
  transfers between devices with their start and end apart: 30 -> 36, of which waited for: 19 -> 19; matrix products, arithmetic and copies ran while one was open for 19% -> 22% of each run, Pallas kernels for 24% -> 21%
where the time goes in v3:
time: 203 us; the launch traced here: 202 us
  waiting for transfers between devices  62.4 us (31%)
  starting transfers between devices  46.8 us (23%)
  Pallas kernels  43.4 us (21%)
  matrix products  18 us (9%)
  local copies, waits for them, and re-layouts  15.6 us (8%)
  other arithmetic  14.9 us (7%)
    pallas_call x1, Pallas kernels, cycle_dot(): pl.pallas_call(functools.partial(cycle_kernel, chips=chips, blocks_in=len...  21.6 us
    dot_general x3, matrix products, ladder_dot(): lax.dot_general(ints, amplitudes, (((0, 1), (0, 1)), ((), ())), preferred...  18 us
    pallas_call x1, Pallas kernels, cycle_layout(): pl.pallas_call(amp_kernel, grid=(virt_col // step,), in_specs=[pl.BlockSp...  17.2 us
    ppermute x1, waiting for transfers between devices, body(): got_most = lax.ppermute(most, 'depth', SWAP_DEPTH)  16.9 us
    ppermute x6, waiting for transfers between devices, reduce_col(): got = [lax.ppermute(b, 'col', shift_x(s + 1)) for s, b in enumerate(sent)]  16.3 us
    ppermute x3, waiting for transfers between devices, up_z(): return lax.ppermute(value, 'row', shift_z(1))  11.7 us
    ppermute x3, starting transfers between devices, down_z(): return lax.ppermute(value, 'row', shift_z(3))  8.17 us
    ppermute x6, starting transfers between devices, reduce_col(): got = [lax.ppermute(b, 'col', shift_x(s + 1)) for s, b in enumerate(sent)]  7.94 us
  transfers between devices with their start and end apart: 36, of which 19 were waited for; matrix products, arithmetic and copies ran while one was open for 22% of the time, Pallas kernels for 21%

profile of v3, /device:TPU:0, one launch (start us, length us, event | category | flops | bytes accessed | tf_op | source)
XLA Modules:
  0.0 202.2 jit_solution(18306358146507498311)
XLA Ops:
  3.9 3.1 %collective-permute-start.1 = (bf16[2464,256]{1,0:T(8,128)(2,1)}, bf16[2464,256]{1,0:T(8,128)(2,1)}, u32[]{:S(2)}, u32[]{:S(2)}) collective-permute-start(bf16[2464,256]{1,0:T(8,128)(2,1)} %bitcast.58), channel_id=1, source_target_pairs={{0,3},{1,2},{2,1},{3,0},{4,7},{5,6},{6,5},{7,4},{8,11},{9,10},{10,... | collective-permute-start | bytes 3784712 | tf_op jit(solution)/shard_map/ppermute | solution.py:231
  7.0 3.7 %slice.22 = bf16[77,77,256]{2,1,0:T(8,128)(2,1)} slice(bf16[77,77,512]{2,1,0:T(8,128)(2,1)} %param.10), slice={[0:77], [0:77], [0:256]} | slice | bytes 6071296 | tf_op jit(solution)/shard_map/slice | solution.py:268
  10.9 17.2 %shard_map.104 = bf16[77,16,2464]{2,1,0:T(8,128)(2,1)} custom-call(bf16[77,77,512]{2,1,0:T(8,128)(2,1)} %src.1), custom_call_target="tpu_custom_call" | custom-call | flops 1000 | bytes 1000 | tf_op jit(solution)/shard_map/pallas_call | solution.py:137
  28.0 3.5 %collective-permute-done.3.refs_6_ = bf16[2464,256]{1,0:T(8,128)(2,1)} collective-permute-done((bf16[2464,256]{1,0:T(8,128)(2,1)}, bf16[2464,256]{1,0:T(8,128)(2,1)}, u32[]{:S(2)}, u32[]{:S(2)}) %collective-permute-start.3) | collective-permute-done | bytes 1261600 | tf_op jit(solution)/shard_map/ppermute | solution.py:232
  34.4 2.8 %collective-permute-start.5 = (bf16[1232,256]{1,0:T(8,128)(2,1)S(1)}, bf16[1232,256]{1,0:T(8,128)(2,1)S(1)}, u32[]{:S(2)}, u32[]{:S(2)}) collective-permute-start(bf16[1232,256]{1,0:T(8,128)(2,1)S(1)} %slice.25), channel_id=1, source_target_pairs={{0,12},{2,14},{4,0},{6,2},{8,4},{10,6},{12,8},{14,10},{1,13},{3,15... | collective-permute-start | bytes 1892360 | tf_op jit(solution)/shard_map/ppermute | solution.py:235
  37.2 4.0 %slice.26 = bf16[77,77,256]{2,1,0:T(8,128)(2,1)} slice(bf16[77,77,512]{2,1,0:T(8,128)(2,1)} %param.10), slice={[0:77], [0:77], [256:512]} | slice | bytes 6071296 | tf_op jit(solution)/shard_map/slice | solution.py:279
  43.0 5.9 %collective-permute-done.4 = bf16[1232,256]{1,0:T(8,128)(2,1)S(1)} collective-permute-done((bf16[1232,256]{1,0:T(8,128)(2,1)S(1)}, bf16[1232,256]{1,0:T(8,128)(2,1)S(1)}, u32[]{:S(2)}, u32[]{:S(2)}) %collective-permute-start.4) | collective-permute-done | bytes 630816 | tf_op jit(solution)/shard_map/ppermute | solution.py:234
  49.4 3.7 %collective-permute-start.6 = (bf16[2464,256]{1,0:T(8,128)(2,1)}, bf16[2464,256]{1,0:T(8,128)(2,1)}, u32[]{:S(2)}, u32[]{:S(2)}) collective-permute-start(bf16[2464,256]{1,0:T(8,128)(2,1)} %collective-permute-done.1.refs_1_), channel_id=1, source_target_pairs={{0,12},{2,14},{4,0},{6,2},{8,4},{10,6},{12,8},{14,10},{1,13},{3,15... | collective-permute-start | bytes 3784712 | tf_op jit(solution)/shard_map/ppermute | solution.py:239
  54.8 3.3 %collective-permute-start.7 = (bf16[2464,256]{1,0:T(8,128)(2,1)}, bf16[2464,256]{1,0:T(8,128)(2,1)}, u32[]{:S(2)}, u32[]{:S(2)}) collective-permute-start(bf16[2464,256]{1,0:T(8,128)(2,1)} %constant_dynamic-update-slice_fusion.refs_4_), channel_id=1, source_target_pairs={{0,3},{1,2},{2,1},{3,0},{4,7},{5,6},{6,5},{7,4},{8,11},{9,10},{10,... | collective-permute-start | bytes 3784712 | tf_op jit(solution)/shard_map/ppermute | solution.py:240
  58.2 6.9 %fusion.4 = f32[512,512,1]{1,0,2:T(8,128)} fusion(bf16[77,77,512]{2,1,0:T(8,128)(2,1)} %param.10, bf16[77,77,512]{2,1,0:T(8,128)(2,1)S(1)} %copy-done), kind=kOutput, calls=%fused_computation.30 | convolution fusion | flops 3108503552 | bytes 13191168 | tf_op jit(solution)/shard_map/dot_general | solution.py:272
  65.3 16.9 %collective-permute-done.refs_9_ = bf16[77,77,256]{2,1,0:T(8,128)(2,1)S(1)} collective-permute-done((bf16[77,77,256]{2,1,0:T(8,128)(2,1)}, bf16[77,77,256]{2,1,0:T(8,128)(2,1)S(1)}, u32[]{:S(2)}, u32[]{:S(2)}) %collective-permute-start) | collective-permute-done | bytes 3035680 | tf_op jit(solution)/shard_map/ppermute | solution.py:269
  83.8 21.6 %shard_map.105 = (f32[616,256]{1,0:T(8,128)S(1)}, f32[616,256]{1,0:T(8,128)S(1)}, f32[616,256]{1,0:T(8,128)}, f32[616,256]{1,0:T(8,128)S(1)}, f32[616,256]{1,0:T...) custom-call(s32[4]{0:T(128)S(1)} %pad_add_fusion.order, ...), custom_call_target="tpu_custom_call" | custom-call | flops 1000 | bytes 1000 | tf_op jit(solution)/shard_map/pallas_call | solution.py:210
  111.0 2.0 collective-permute-start.10
  113.0 2.4 %collective-permute-start.12 = (f32[616,256]{1,0:T(8,128)S(1)}, f32[616,256]{1,0:T(8,128)S(1)}, u32[]{:S(2)}, u32[]{:S(2)}) collective-permute-start(f32[616,256]{1,0:T(8,128)S(1)} %add.188), channel_id=1, source_target_pairs={{0,96},{16,112},{32,0},{48,16},{64,32},{80,48},{96,64},{112,80},{1... | collective-permute-start | bytes 1892360 | tf_op jit(solution)/shard_map/ppermute | solution.py:67
  115.4 4.7 %fusion.5 = f32[256,512,1]{1,0,2:T(8,128)S(1)} fusion(bf16[77,77,256]{2,1,0:T(8,128)(2,1)S(1)} %copy-done.2, bf16[77,77,512]{2,1,0:T(8,128)(2,1)} %src.1), kind=kOutput, calls=%fused_computation.31 | convolution fusion | flops 1554251776 | bytes 9631232 | tf_op jit(solution)/shard_map/dot_general | solution.py:272
  121.5 2.0 add.190.refs_3_
  123.5 2.0 add.189.refs_2_
  125.5 4.2 %collective-permute-done.10.refs_0_ = f32[616,256]{1,0:T(8,128)S(1)} collective-permute-done((f32[616,256]{1,0:T(8,128)S(1)}, f32[616,256]{1,0:T(8,128)S(1)}, u32[]{:S(2)}, u32[]{:S(2)}) %collective-permute-start.10) | collective-permute-done | bytes 630816 | tf_op jit(solution)/shard_map/ppermute | solution.py:63
  131.3 2.7 %shard_map.106 = (f32[6,2,16,512]{3,2,1,0:T(8,128)}, f32[6,2,16,512]{3,2,1,0:T(8,128)}, f32[6,2,16,512]{3,2,1,0:T(8,128)}, f32[6,2,16,512]{3,2,1,0:T(8,128)}) custom-call(s32[1]{0:T(128)} %bitcast.start, f32[6,4,2,16,512]{4,3,2,1,0:T(8,128)} %pad_maximum_fusion.src, f32[616,256]{1,0:T(8,128)} %copy-done.6, f32[616,256]{1,0:T(8,128)} %copy-done.4, ...), custom_call_target="tpu_custom_call" | custom-call | flops 1000 | bytes 1000 | tf_op jit(solution)/shard_map/pallas_call | solution.py:83
  134.3 4.2 %collective-permute-start.16 = (f32[6,2,16,512]{3,2,1,0:T(8,128)}, f32[6,2,16,512]{3,2,1,0:T(8,128)S(1)}, u32[]{:S(2)}, u32[]{:S(2)}) collective-permute-start(f32[6,2,16,512]{3,2,1,0:T(8,128)} %get-tuple-element.43), channel_id=1, source_target_pairs={{0,8},{2,10},{4,12},{6,14},{8,0},{10,2},{12,4},{14,6},{1,9},{3,11}... | collective-permute-start | bytes 1179656 | tf_op jit(solution)/shard_map/ppermute | solution.py:100
  140.0 2.5 %collective-permute-start.25 = (f32[616,256]{1,0:T(8,128)S(1)}, f32[616,256]{1,0:T(8,128)S(1)}, u32[]{:S(2)}, u32[]{:S(2)}) collective-permute-start(f32[616,256]{1,0:T(8,128)S(1)} %copy-done.8), channel_id=1, source_target_pairs={{0,96},{16,112},{32,0},{48,16},{64,32},{80,48},{96,64},{112,80},{1... | collective-permute-start | bytes 1892360 | tf_op jit(solution)/shard_map/ppermute | solution.py:67
  142.6 3.8 %collective-permute-done.15 = f32[6,2,16,512]{3,2,1,0:T(8,128)S(1)} collective-permute-done((f32[6,2,16,512]{3,2,1,0:T(8,128)}, f32[6,2,16,512]{3,2,1,0:T(8,128)S(1)}, u32[]{:S(2)}, u32[]{:S(2)}) %collective-permute-start.15) | collective-permute-done | bytes 393248 | tf_op jit(solution)/shard_map/ppermute | solution.py:100
  146.9 9.0 %collective-permute-done.16 = f32[6,2,16,512]{3,2,1,0:T(8,128)S(1)} collective-permute-done((f32[6,2,16,512]{3,2,1,0:T(8,128)}, f32[6,2,16,512]{3,2,1,0:T(8,128)S(1)}, u32[]{:S(2)}, u32[]{:S(2)}) %collective-permute-start.16) | collective-permute-done | bytes 393248 | tf_op jit(solution)/shard_map/ppermute | solution.py:100
  155.9 3.2 %collective-permute-start.23 = (f32[616,256]{1,0:T(8,128)S(1)}, f32[616,256]{1,0:T(8,128)S(1)}, u32[]{:S(2)}, u32[]{:S(2)}) collective-permute-start(f32[616,256]{1,0:T(8,128)S(1)} %add_add_fusion.2), channel_id=1, source_target_pairs={{0,96},{16,112},{32,0},{48,16},{64,32},{80,48},{96,64},{112,80},{1... | collective-permute-start | bytes 1892360 | tf_op jit(solution)/shard_map/ppermute | solution.py:67
  159.3 2.0 collective-permute-start.18
  161.3 6.4 %fusion.6 = f32[256,512,1]{1,0,2:T(8,128)} fusion(bf16[77,77,256]{2,1,0:T(8,128)(2,1)} %collective-permute-done.19, bf16[77,77,512]{2,1,0:T(8,128)(2,1)} %src.1), kind=kOutput, calls=%fused_computation.32 | convolution fusion | flops 1554251776 | bytes 9631232 | tf_op jit(solution)/shard_map/dot_general | solution.py:272
  168.4 7.5 %collective-permute-done.21.refs_1_ = f32[616,256]{1,0:T(8,128)S(1)} collective-permute-done((f32[616,256]{1,0:T(8,128)S(1)}, f32[616,256]{1,0:T(8,128)S(1)}, u32[]{:S(2)}, u32[]{:S(2)}) %collective-permute-start.21) | collective-permute-done | bytes 630816 | tf_op jit(solution)/shard_map/ppermute | solution.py:63
  177.0 2.0 shard_map.107
  178.9 3.3 %collective-permute-start.27 = (f32[2,2,16,512]{3,2,1,0:T(8,128)}, f32[2,2,16,512]{3,2,1,0:T(8,128)S(1)}, u32[]{:S(2)}, u32[]{:S(2)}) collective-permute-start(f32[2,2,16,512]{3,2,1,0:T(8,128)} %get-tuple-element.52), channel_id=1, source_target_pairs={{0,8},{2,10},{4,12},{6,14},{8,0},{10,2},{12,4},{14,6},{1,9},{3,11}... | collective-permute-start | bytes 393224 | tf_op jit(solution)/shard_map/ppermute | solution.py:100
  187.7 2.0 collective-permute-start.29
  191.1 2.5 %collective-permute-done.29 = f32[2,16,512]{2,1,0:T(8,128)S(1)} collective-permute-done((f32[2,16,512]{2,1,0:T(8,128)S(1)}, f32[2,16,512]{2,1,0:T(8,128)S(1)}, u32[]{:S(2)}, u32[]{:S(2)}) %collective-permute-start.29) | collective-permute-done | bytes 65568 | tf_op jit(solution)/shard_map/ppermute | solution.py:102
  195.2 2.0 collective-permute-start.32
  (146 shorter events, 38.1 us)
Async XLA Ops:
  0.6 31.0 %collective-permute-start.3 = (bf16[2464,256]{1,0:T(8,128)(2,1)}, bf16[2464,256]{1,0:T(8,128)(2,1)}, u32[]{:S(2)}, u32[]{:S(2)}) collective-permute-start(bf16[2464,256]{1,0:T(8,128)(2,1)} %bitcast.56), channel_id=1, source_target_pairs={{0,4},{2,6},{4,8},{6,10},{8,12},{10,14},{12,0},{14,2},{1,5},{3,7},... | collective-permute-start | bytes 3784712 | tf_op jit(solution)/shard_map/ppermute | solution.py:232
  2.3 31.0 %collective-permute-start.2 = (bf16[2464,256]{1,0:T(8,128)(2,1)}, bf16[2464,256]{1,0:T(8,128)(2,1)}, u32[]{:S(2)}, u32[]{:S(2)}) collective-permute-start(bf16[2464,256]{1,0:T(8,128)(2,1)} %bitcast.57), channel_id=1, source_target_pairs={{0,12},{2,14},{4,0},{6,2},{8,4},{10,6},{12,8},{14,10},{1,13},{3,15... | collective-permute-start | bytes 3784712 | tf_op jit(solution)/shard_map/ppermute | solution.py:233
  3.9 33.3 %collective-permute-start.1 = (bf16[2464,256]{1,0:T(8,128)(2,1)}, bf16[2464,256]{1,0:T(8,128)(2,1)}, u32[]{:S(2)}, u32[]{:S(2)}) collective-permute-start(bf16[2464,256]{1,0:T(8,128)(2,1)} %bitcast.58), channel_id=1, source_target_pairs={{0,3},{1,2},{2,1},{3,0},{4,7},{5,6},{6,5},{7,4},{8,11},{9,10},{10,... | collective-permute-start | bytes 3784712 | tf_op jit(solution)/shard_map/ppermute | solution.py:231
  10.7 71.4 %collective-permute-start = (bf16[77,77,256]{2,1,0:T(8,128)(2,1)}, bf16[77,77,256]{2,1,0:T(8,128)(2,1)S(1)}, u32[]{:S(2)}, u32[]{:S(2)}) collective-permute-start(bf16[77,77,256]{2,1,0:T(8,128)(2,1)} %slice.22), channel_id=1, source_target_pairs={{0,1},{1,0},{2,3},{3,2},{4,5},{5,4},{6,7},{7,6},{8,9},{9,8},{10,11... | collective-permute-start | bytes 9106952 | tf_op jit(solution)/shard_map/ppermute | solution.py:269
  32.7 16.2 %collective-permute-start.4 = (bf16[1232,256]{1,0:T(8,128)(2,1)S(1)}, bf16[1232,256]{1,0:T(8,128)(2,1)S(1)}, u32[]{:S(2)}, u32[]{:S(2)}) collective-permute-start(bf16[1232,256]{1,0:T(8,128)(2,1)S(1)} %slice.24), channel_id=1, source_target_pairs={{0,4},{2,6},{4,8},{6,10},{8,12},{10,14},{12,0},{14,2},{1,5},{3,7},... | collective-permute-start | bytes 1892360 | tf_op jit(solution)/shard_map/ppermute | solution.py:234
  34.4 15.0 %collective-permute-start.5 = (bf16[1232,256]{1,0:T(8,128)(2,1)S(1)}, bf16[1232,256]{1,0:T(8,128)(2,1)S(1)}, u32[]{:S(2)}, u32[]{:S(2)}) collective-permute-start(bf16[1232,256]{1,0:T(8,128)(2,1)S(1)} %slice.25), channel_id=1, source_target_pairs={{0,12},{2,14},{4,0},{6,2},{8,4},{10,6},{12,8},{14,10},{1,13},{3,15... | collective-permute-start | bytes 1892360 | tf_op jit(solution)/shard_map/ppermute | solution.py:235
  41.2 118.1 %collective-permute-start.19 = (bf16[77,77,256]{2,1,0:T(8,128)(2,1)}, bf16[77,77,256]{2,1,0:T(8,128)(2,1)}, u32[]{:S(2)}, u32[]{:S(2)}) collective-permute-start(bf16[77,77,256]{2,1,0:T(8,128)(2,1)} %slice.26), channel_id=1, source_target_pairs={{0,1},{1,0},{2,3},{3,2},{4,5},{5,4},{6,7},{7,6},{8,9},{9,8},{10,11... | collective-permute-start | bytes 9106952 | tf_op jit(solution)/shard_map/ppermute | solution.py:280
  49.4 32.8 %collective-permute-start.6 = (bf16[2464,256]{1,0:T(8,128)(2,1)}, bf16[2464,256]{1,0:T(8,128)(2,1)}, u32[]{:S(2)}, u32[]{:S(2)}) collective-permute-start(bf16[2464,256]{1,0:T(8,128)(2,1)} %collective-permute-done.1.refs_1_), channel_id=1, source_target_pairs={{0,12},{2,14},{4,0},{6,2},{8,4},{10,6},{12,8},{14,10},{1,13},{3,15... | collective-permute-start | bytes 3784712 | tf_op jit(solution)/shard_map/ppermute | solution.py:239
  53.1 29.1 %collective-permute-start.8 = (bf16[2464,256]{1,0:T(8,128)(2,1)}, bf16[2464,256]{1,0:T(8,128)(2,1)}, u32[]{:S(2)}, u32[]{:S(2)}) collective-permute-start(bf16[2464,256]{1,0:T(8,128)(2,1)} %collective-permute-done.1.refs_1_), channel_id=1, source_target_pairs={{0,4},{2,6},{4,8},{6,10},{8,12},{10,14},{12,0},{14,2},{1,5},{3,7},... | collective-permute-start | bytes 3784712 | tf_op jit(solution)/shard_map/ppermute | solution.py:238
  54.8 29.0 %collective-permute-start.7 = (bf16[2464,256]{1,0:T(8,128)(2,1)}, bf16[2464,256]{1,0:T(8,128)(2,1)}, u32[]{:S(2)}, u32[]{:S(2)}) collective-permute-start(bf16[2464,256]{1,0:T(8,128)(2,1)} %constant_dynamic-update-slice_fusion.refs_4_), channel_id=1, source_target_pairs={{0,3},{1,2},{2,1},{3,0},{4,7},{5,6},{6,5},{7,4},{8,11},{9,10},{10,... | collective-permute-start | bytes 3784712 | tf_op jit(solution)/shard_map/ppermute | solution.py:240
  105.5 5.5 %collective-permute-start.14 = (f32[616,256]{1,0:T(8,128)}, f32[616,256]{1,0:T(8,128)}, u32[]{:S(2)}, u32[]{:S(2)}) collective-permute-start(f32[616,256]{1,0:T(8,128)} %get-tuple-element.40), channel_id=1, source_target_pairs={{0,16},{16,0},{32,48},{48,32},{64,80},{80,64},{96,112},{112,96},{1... | collective-permute-start | bytes 1892360 | tf_op jit(solution)/shard_map/ppermute | solution.py:59
  106.1 6.9 %collective-permute-start.13 = (f32[616,256]{1,0:T(8,128)}, f32[616,256]{1,0:T(8,128)}, u32[]{:S(2)}, u32[]{:S(2)}) collective-permute-start(f32[616,256]{1,0:T(8,128)} %get-tuple-element.38), channel_id=1, source_target_pairs={{0,16},{16,0},{32,48},{48,32},{64,80},{80,64},{96,112},{112,96},{1... | collective-permute-start | bytes 1892360 | tf_op jit(solution)/shard_map/ppermute | solution.py:59
  107.9 30.6 %collective-permute-start.20 = (f32[616,256]{1,0:T(8,128)}, f32[616,256]{1,0:T(8,128)}, u32[]{:S(2)}, u32[]{:S(2)}) collective-permute-start(f32[616,256]{1,0:T(8,128)} %get-tuple-element.47), channel_id=1, source_target_pairs={{0,16},{16,0},{32,48},{48,32},{64,80},{80,64},{96,112},{112,96},{1... | collective-permute-start | bytes 1892360 | tf_op jit(solution)/shard_map/ppermute | solution.py:59
  109.5 30.4 %collective-permute-start.22 = (f32[616,256]{1,0:T(8,128)}, f32[616,256]{1,0:T(8,128)S(1)}, u32[]{:S(2)}, u32[]{:S(2)}) collective-permute-start(f32[616,256]{1,0:T(8,128)} %get-tuple-element.49), channel_id=1, source_target_pairs={{0,16},{16,0},{32,48},{48,32},{64,80},{80,64},{96,112},{112,96},{1... | collective-permute-start | bytes 1892360 | tf_op jit(solution)/shard_map/ppermute | solution.py:59
  111.0 18.7 %collective-permute-start.10 = (f32[616,256]{1,0:T(8,128)S(1)}, f32[616,256]{1,0:T(8,128)S(1)}, u32[]{:S(2)}, u32[]{:S(2)}) collective-permute-start(f32[616,256]{1,0:T(8,128)S(1)} %add.187), channel_id=1, source_target_pairs={{0,32},{16,48},{32,64},{48,80},{64,96},{80,112},{96,0},{112,16},{1... | collective-permute-start | bytes 1892360 | tf_op jit(solution)/shard_map/ppermute | solution.py:63
  113.0 16.7 %collective-permute-start.12 = (f32[616,256]{1,0:T(8,128)S(1)}, f32[616,256]{1,0:T(8,128)S(1)}, u32[]{:S(2)}, u32[]{:S(2)}) collective-permute-start(f32[616,256]{1,0:T(8,128)S(1)} %add.188), channel_id=1, source_target_pairs={{0,96},{16,112},{32,0},{48,16},{64,32},{80,48},{96,64},{112,80},{1... | collective-permute-start | bytes 1892360 | tf_op jit(solution)/shard_map/ppermute | solution.py:67
  134.1 12.3 %collective-permute-start.15 = (f32[6,2,16,512]{3,2,1,0:T(8,128)}, f32[6,2,16,512]{3,2,1,0:T(8,128)S(1)}, u32[]{:S(2)}, u32[]{:S(2)}) collective-permute-start(f32[6,2,16,512]{3,2,1,0:T(8,128)} %get-tuple-element.42), channel_id=1, source_target_pairs={{0,4},{2,6},{4,8},{6,10},{8,12},{10,14},{12,0},{14,2},{1,5},{3,7},... | collective-permute-start | bytes 1179656 | tf_op jit(solution)/shard_map/ppermute | solution.py:100
  134.3 21.5 %collective-permute-start.16 = (f32[6,2,16,512]{3,2,1,0:T(8,128)}, f32[6,2,16,512]{3,2,1,0:T(8,128)S(1)}, u32[]{:S(2)}, u32[]{:S(2)}) collective-permute-start(f32[6,2,16,512]{3,2,1,0:T(8,128)} %get-tuple-element.43), channel_id=1, source_target_pairs={{0,8},{2,10},{4,12},{6,14},{8,0},{10,2},{12,4},{14,6},{1,9},{3,11}... | collective-permute-start | bytes 1179656 | tf_op jit(solution)/shard_map/ppermute | solution.py:100
  138.6 17.3 %collective-permute-start.17 = (f32[6,2,16,512]{3,2,1,0:T(8,128)}, f32[6,2,16,512]{3,2,1,0:T(8,128)S(1)}, u32[]{:S(2)}, u32[]{:S(2)}) collective-permute-start(f32[6,2,16,512]{3,2,1,0:T(8,128)} %get-tuple-element.44), channel_id=1, source_target_pairs={{0,12},{2,14},{4,0},{6,2},{8,4},{10,6},{12,8},{14,10},{1,13},{3,15... | collective-permute-start | bytes 1179656 | tf_op jit(solution)/shard_map/ppermute | solution.py:100
  140.0 27.8 %collective-permute-start.25 = (f32[616,256]{1,0:T(8,128)S(1)}, f32[616,256]{1,0:T(8,128)S(1)}, u32[]{:S(2)}, u32[]{:S(2)}) collective-permute-start(f32[616,256]{1,0:T(8,128)S(1)} %copy-done.8), channel_id=1, source_target_pairs={{0,96},{16,112},{32,0},{48,16},{64,32},{80,48},{96,64},{112,80},{1... | collective-permute-start | bytes 1892360 | tf_op jit(solution)/shard_map/ppermute | solution.py:67
  146.4 22.0 %collective-permute-start.24 = (f32[616,256]{1,0:T(8,128)S(1)}, f32[616,256]{1,0:T(8,128)S(1)}, u32[]{:S(2)}, u32[]{:S(2)}) collective-permute-start(f32[616,256]{1,0:T(8,128)S(1)} %copy-done.7), channel_id=1, source_target_pairs={{0,32},{16,48},{32,64},{48,80},{64,96},{80,112},{96,0},{112,16},{1... | collective-permute-start | bytes 1892360 | tf_op jit(solution)/shard_map/ppermute | solution.py:63
  155.9 20.0 %collective-permute-start.21 = (f32[616,256]{1,0:T(8,128)S(1)}, f32[616,256]{1,0:T(8,128)S(1)}, u32[]{:S(2)}, u32[]{:S(2)}) collective-permute-start(f32[616,256]{1,0:T(8,128)S(1)} %add_add_fusion.3), channel_id=1, source_target_pairs={{0,32},{16,48},{32,64},{48,80},{64,96},{80,112},{96,0},{112,16},{1... | collective-permute-start | bytes 1892360 | tf_op jit(solution)/shard_map/ppermute | solution.py:63
  155.9 20.0 %collective-permute-start.23 = (f32[616,256]{1,0:T(8,128)S(1)}, f32[616,256]{1,0:T(8,128)S(1)}, u32[]{:S(2)}, u32[]{:S(2)}) collective-permute-start(f32[616,256]{1,0:T(8,128)S(1)} %add_add_fusion.2), channel_id=1, source_target_pairs={{0,96},{16,112},{32,0},{48,16},{64,32},{80,48},{96,64},{112,80},{1... | collective-permute-start | bytes 1892360 | tf_op jit(solution)/shard_map/ppermute | solution.py:67
  159.3 8.4 %collective-permute-start.18 = (f32[6,16,512]{2,1,0:T(8,128)S(1)}, f32[6,16,512]{2,1,0:T(8,128)S(1)}, u32[]{:S(2)}, u32[]{:S(2)}) collective-permute-start(f32[6,16,512]{2,1,0:T(8,128)S(1)} %dynamic-slice_bitcast_fusion), channel_id=1, source_target_pairs={{0,2},{2,0},{4,6},{6,4},{8,10},{10,8},{12,14},{14,12},{1,3},{3,1},... | collective-permute-start | bytes 589832 | tf_op jit(solution)/shard_map/ppermute | solution.py:102
  167.7 14.7 %collective-permute-start.34 = (f32[616,256]{1,0:T(8,128)}, f32[616,256]{1,0:T(8,128)}, u32[]{:S(2)}, u32[]{:S(2)}) collective-permute-start(f32[616,256]{1,0:T(8,128)} %get-tuple-element.55), channel_id=1, source_target_pairs={{0,16},{16,0},{32,48},{48,32},{64,80},{80,64},{96,112},{112,96},{1... | collective-permute-start | bytes 1892360 | tf_op jit(solution)/shard_map/ppermute | solution.py:59
  167.8 21.9 %collective-permute-start.35 = (f32[616,256]{1,0:T(8,128)}, f32[616,256]{1,0:T(8,128)}, u32[]{:S(2)}, u32[]{:S(2)}) collective-permute-start(f32[616,256]{1,0:T(8,128)} %get-tuple-element.57), channel_id=1, source_target_pairs={{0,16},{16,0},{32,48},{48,32},{64,80},{80,64},{96,112},{112,96},{1... | collective-permute-start | bytes 1892360 | tf_op jit(solution)/shard_map/ppermute | solution.py:59
  178.9 6.4 %collective-permute-start.26 = (f32[2,2,16,512]{3,2,1,0:T(8,128)}, f32[2,2,16,512]{3,2,1,0:T(8,128)S(1)}, u32[]{:S(2)}, u32[]{:S(2)}) collective-permute-start(f32[2,2,16,512]{3,2,1,0:T(8,128)} %get-tuple-element.51), channel_id=1, source_target_pairs={{0,4},{2,6},{4,8},{6,10},{8,12},{10,14},{12,0},{14,2},{1,5},{3,7},... | collective-permute-start | bytes 393224 | tf_op jit(solution)/shard_map/ppermute | solution.py:100
  178.9 7.9 %collective-permute-start.27 = (f32[2,2,16,512]{3,2,1,0:T(8,128)}, f32[2,2,16,512]{3,2,1,0:T(8,128)S(1)}, u32[]{:S(2)}, u32[]{:S(2)}) collective-permute-start(f32[2,2,16,512]{3,2,1,0:T(8,128)} %get-tuple-element.52), channel_id=1, source_target_pairs={{0,8},{2,10},{4,12},{6,14},{8,0},{10,2},{12,4},{14,6},{1,9},{3,11}... | collective-permute-start | bytes 393224 | tf_op jit(solution)/shard_map/ppermute | solution.py:100
  182.2 5.4 %collective-permute-start.28 = (f32[2,2,16,512]{3,2,1,0:T(8,128)}, f32[2,2,16,512]{3,2,1,0:T(8,128)S(1)}, u32[]{:S(2)}, u32[]{:S(2)}) collective-permute-start(f32[2,2,16,512]{3,2,1,0:T(8,128)} %get-tuple-element.53), channel_id=1, source_target_pairs={{0,12},{2,14},{4,0},{6,2},{8,4},{10,6},{12,8},{14,10},{1,13},{3,15... | collective-permute-start | bytes 393224 | tf_op jit(solution)/shard_map/ppermute | solution.py:100
  187.7 5.8 %collective-permute-start.29 = (f32[2,16,512]{2,1,0:T(8,128)S(1)}, f32[2,16,512]{2,1,0:T(8,128)S(1)}, u32[]{:S(2)}, u32[]{:S(2)}) collective-permute-start(f32[2,16,512]{2,1,0:T(8,128)S(1)} %dynamic-slice_bitcast_fusion.2), channel_id=1, source_target_pairs={{0,2},{2,0},{4,6},{6,4},{8,10},{10,8},{12,14},{14,12},{1,3},{3,1},... | collective-permute-start | bytes 196616 | tf_op jit(solution)/shard_map/ppermute | solution.py:102
  195.1 5.2 %collective-permute-start.31 = (f32[16,512]{1,0:T(8,128)S(1)}, f32[16,512]{1,0:T(8,128)S(1)}, u32[]{:S(2)}, u32[]{:S(2)}) collective-permute-start(f32[16,512]{1,0:T(8,128)S(1)} %get-tuple-element.58), channel_id=1, source_target_pairs={{0,32},{16,48},{32,64},{48,80},{64,96},{80,112},{96,0},{112,16},{1... | collective-permute-start | bytes 98312 | tf_op jit(solution)/shard_map/ppermute | solution.py:54
  195.2 5.5 %collective-permute-start.32 = (f32[16,512]{1,0:T(8,128)S(1)}, f32[16,512]{1,0:T(8,128)S(1)}, u32[]{:S(2)}, u32[]{:S(2)}) collective-permute-start(f32[16,512]{1,0:T(8,128)S(1)} %get-tuple-element.60), channel_id=1, source_target_pairs={{0,64},{16,80},{32,96},{48,112},{64,0},{80,16},{96,32},{112,48},{1... | collective-permute-start | bytes 98312 | tf_op jit(solution)/shard_map/ppermute | solution.py:54
  (35 other events, 221.3 us)
